TPU v7x, 512 devices: a whole 4x8x8 slice. The times are simulated.
512 devices in a mesh: band: 64 (over z, x, core), mem: 8 (over y).
Axes of the slice: x: 4, y: 8, z: 8, core: 2. Of those that a mesh axis runs over, the one named last changes fastest.
Arguments:
- spectra: bfloat16 [16, 4, 2, 2, 901120], P('mem', None, None, None, 'band'), may hold values from -6 to 6
- legendre: bfloat16 [40, 901120], P(None, 'band'), may hold values from -0.0034179688 to 0.0034179688
- pair_waves: int32 [640], P('band'), may hold values from 0 to 639, each once
- band_lengths: int32 [64], replicated, may hold values from 1 to 2, 80 in all
- eof_basis: bfloat16 [128, 2560, 256], P('band'), may hold values from -0.0390625 to 0.0390625
Outputs:
- grid_fields: bfloat16 [16, 4, 2, 128, 2560], P('mem', None, None, 'band')
- eof_coeffs: float32 [16, 4, 2, 256], P('mem', None, None, 'band')
Inputs may be any that keep to these rules, and one draw needn't show every extreme that they name: `pair_waves`: every lower wavenumber 0 .. 639 stands in exactly one pair slot. `band_lengths`: the lengths sum to 80; some band has exactly 2 rows.
All inputs are finite; a program needn't handle non-finite values.
Results may differ from a plain program's by a relative error of at most 0.0055.
Values may be sent and summed in bfloat16 or wider, within the bound.
No kernel may reach another device: no remote copies, remote signals or barrier semaphores. Data moves between devices by JAX's collectives and lax.ppermute only.
A program may use at most 192 MiB of HBM per device.

v0:
```python
import math

import jax
import jax.numpy as jnp
from jax import lax
from jax.sharding import PartitionSpec as P

WAVE_COUNT = 1280
BLK = 128


def wave_block(orders, start, width, length):
    lon_index = start + jnp.arange(width, dtype=jnp.int32)
    phase_idx = orders[..., None] * lon_index % length
    angle_rad = phase_idx.astype(jnp.float32) * (2.0 * math.pi / length)
    weight = jnp.where(orders == 0, 1.0, 2.0).astype(jnp.float32)[..., None]
    return jnp.stack([weight * jnp.cos(angle_rad), -weight * jnp.sin(angle_rad)]).astype(
        jnp.bfloat16
    )


def shards(spectra, legendre, pair_waves, band_lengths, eof_basis):
    ens_dev, fields, level_stack, re_im, slot_count = spectra.shape
    lat_half = legendre.shape[0]
    pairs_dev = pair_waves.shape[0]
    blocks = slot_count // (pairs_dev * BLK)
    columns = ens_dev * fields * level_stack * re_im
    band_count = lax.axis_size("band")
    most_rows, longitudes, eof_modes = eof_basis.shape
    spectral_data = spectra.reshape(columns, pairs_dev, blocks, BLK)
    legendre_rows = legendre.reshape(lat_half, pairs_dev, blocks, BLK)
    position = jnp.arange(blocks * BLK, dtype=jnp.int32).reshape(1, blocks, BLK)
    lower_wave = pair_waves.reshape(pairs_dev, 1, 1)
    low_blocks = WAVE_COUNT // BLK - lower_wave // BLK
    upper_pos = position - low_blocks * BLK
    in_range = (position < WAVE_COUNT - lower_wave) | (upper_pos >= 0) & (
        upper_pos < lower_wave + 1
    )
    spectral_data = spectral_data * in_range.astype(jnp.bfloat16)[None]
    block_index = jnp.arange(blocks, dtype=jnp.int32)[None, :]
    low_owner = (block_index < low_blocks[:, :, 0]).astype(jnp.float32)
    owners = jnp.stack([low_owner, 1.0 - low_owner], axis=1)
    alternate = jnp.where(jnp.arange(BLK) % 2 == 0, 1.0, -1.0).astype(jnp.bfloat16)
    north_part = jnp.einsum(
        "cptk,jptk->ptcj", spectral_data, legendre_rows, preferred_element_type=jnp.float32
    )
    south_part = jnp.einsum(
        "cptk,jptk->ptcj",
        spectral_data,
        legendre_rows * alternate,
        preferred_element_type=jnp.float32,
    )
    rows_all = jnp.concatenate([north_part, south_part[..., ::-1]], axis=-1)
    fourier = jnp.einsum(
        "pht,ptcj->jphc", owners, rows_all, precision=lax.Precision.HIGHEST
    ).astype(jnp.bfloat16)
    starts = jnp.cumsum(band_lengths) - band_lengths
    offsets = jnp.arange(most_rows, dtype=jnp.int32)
    row_index = jnp.minimum(starts[:, None] + offsets[None, :], 2 * lat_half - 1).reshape(-1)
    packed = jnp.take(fourier, row_index, axis=0).reshape(
        band_count, most_rows, pairs_dev * 2 * columns
    )
    arrived = lax.all_to_all(packed, "band", split_axis=0, concat_axis=0, tiled=True)
    all_waves = lax.all_gather(pair_waves, "band", axis=0, tiled=True).reshape(
        band_count, pairs_dev
    )
    lower_all = all_waves.T
    orders = jnp.stack([lower_all, WAVE_COUNT - 1 - lower_all], axis=1)
    arrived = arrived.reshape(
        band_count, most_rows, pairs_dev, 2, ens_dev, fields, level_stack, re_im
    )
    lon_width = math.gcd(longitudes, 512)
    lon_blocks = longitudes // lon_width

    def synth_block(block_number):
        table_part = wave_block(orders, block_number * lon_width, lon_width, longitudes)
        return jnp.einsum(
            "srphabdc,cphsk->abdrk", arrived, table_part, preferred_element_type=jnp.float32
        )

    grid_parts = lax.map(synth_block, jnp.arange(lon_blocks, dtype=jnp.int32))
    grid_sum = jnp.moveaxis(grid_parts, 0, 4).reshape(
        ens_dev, fields, level_stack, most_rows, longitudes
    )
    own_rows = band_lengths[lax.axis_index("band")]
    row_keep = (offsets < own_rows).astype(jnp.float32)
    grid_fields = (grid_sum * row_keep[:, None]).astype(jnp.bfloat16)
    flat_grid = grid_fields.reshape(ens_dev * fields * level_stack, most_rows * longitudes)
    partial_value = jnp.dot(
        flat_grid,
        eof_basis.reshape(most_rows * longitudes, eof_modes),
        preferred_element_type=jnp.float32,
    )
    share_width = eof_modes // band_count
    summed_all = lax.psum(partial_value, "band")
    own_share = lax.dynamic_slice_in_dim(
        summed_all, lax.axis_index("band") * share_width, share_width, 1
    )
    local_share = own_share.reshape(ens_dev, fields * level_stack, share_width)
    summed = lax.psum(jnp.sum(local_share, axis=0), "mem")
    anomaly = local_share - summed / (ens_dev * lax.axis_size("mem"))
    return (grid_fields, anomaly.reshape(ens_dev, fields, level_stack, share_width))


def solution(mesh):
    return jax.shard_map(
        shards,
        mesh=mesh,
        in_specs=(
            P("mem", None, None, None, "band"),
            P(None, "band"),
            P("band"),
            P(),
            P("band", None, None),
        ),
        out_specs=(P("mem", None, None, "band", None), P("mem", None, None, "band")),
        check_vma=False,
    )
```

profile of v0, /device:TPU:1, one launch (start us, length us, event | category | flops | bytes accessed | tf_op | source)
XLA Modules:
  0.0 399.7 jit_solution(17721014867123769294)
XLA Ops:
  0.7 0.8 broadcast_subtract_fusion.2
  1.5 0.1 broadcast_subtract_fusion.1
  1.6 0.1 compare_convert_fusion
  1.7 0.7 copy.36
  2.4 0.1 reduce-window.9
  2.5 0.1 reduce
  2.6 0.7 sub.62
  3.3 2.6 reshape.297
  5.9 3.4 reshape.301
  9.3 0.1 fusion.26
  9.4 1.5 broadcast_multiply_fusion.1
  10.9 0.2 copy-done.1
  11.1 0.1 broadcast_multiply_fusion
  11.2 2.0 fusion.20
  13.2 2.0 fusion.18
  15.2 4.0 rev.3
  19.2 2.6 pad_maximum_fusion
  21.8 3.3 fusion.15
  25.1 0.4 copy.44
  25.5 0.1 copy.43
  25.6 0.1 min.22
  25.8 2.7 gather_fusion
  28.5 1.8 gather.7
  30.2 0.1 copy.37
  30.4 0.9 broadcast_select_fusion
  31.3 14.8 %all-to-all-start = ((bf16[64,2,640]{2,1,0:T(2,128)(2,1)}), bf16[64,2,640]{2,1,0:T(2,128)(2,1)S(1)}, u32[]{:S(2)}, u32[]{:S(2)}) async-start(bf16[64,2,640]{2,1,0:T(2,128)(2,1)} %broadcast_select_fusion), calls=%async_computation | async-start | bytes 327680 | tf_op jit(solution)/shard_map/all_to_all | solution.py:63
  46.1 1.3 dynamic-slice
  48.2 0.2 dynamic-update-slice
  48.4 17.0 %all-reduce = s32[640]{0:T(1024)S(1)} all-reduce(s32[640]{0:T(1024)S(1)} %dynamic-update-slice), channel_id=1, replica_groups=mesh['band'=64,'mem'=8] {'band'}, use_global_device_ids=true, to_apply=%add | all-reduce | flops 640 | bytes 5120
  65.4 0.1 reshape.294
  65.6 0.1 copy.35
  65.8 0.7 dynamic_slice.13
  66.5 0.7 compare_convert_fusion.1
  67.2 0.3 copy.45
  67.4 0.8 copy.47
  68.3 68.8 %while.12 = (s32[]{:T(128)}, f32[5,2,4,2,2,512]{5,2,3,1,4,0:T(4,128)S(1)}, s32[10,2,64]{2,0,1:T(8,128)S(1)}, s32[5]{0:T(128)S(1)}, bf16[64,2,10,2,2,4,2,2]{0,5,2,3,7,6,4,1:T(4,128)(2,1)}, /*index=5*/s32[]{:T(128)}, s32[1]{0:T(128)}) while((s32[]{:T(128)}, f32[5,2,4,2,2,512]{5,2,3,1,4,0:T(4,128)S(1)}, s32[10,2,64]{2,0,1:T(8,128)S(1)}, ...), condition=%wide.region_2.3_spmd, body=%wide.region_1.2_spmd.sunk | while | flops 97652992 | bytes 6326409 | solution.py:81
  68.3 0.6 dynamic_slice.17
  69.5 11.9 %multiply_convert_fusion.5 = (bf16[1,10,2,64,512]{4,3,1,2,0:T(8,128)(2,1)S(1)}, bf16[1,10,2,64,512]{4,3,1,2,0:T(8,128)(2,1)S(1)}) fusion(s32[512]{0:T(512)S(1)} %iota_add_fusion.2, s32[10,2,64]{2,0,1:T(8,128)S(1)} %get-tuple-element.159, f32[10,2,64]{2,0,1:T(8,128)S(1)} %get-tuple-element.139, f32[10,2,64]{2,0,1:T(8,128)S(1)} %get-tuple-element.140), kind=kLoop, calls=%fused_computation.6.clone.1 | loop fusion | flops 8519680 | bytes 2638848 | tf_op jit(solution)/shard_map/convert
  81.4 0.6 fusion.42
  82.0 0.6 dynamic_slice.17
  83.3 11.9 %multiply_convert_fusion.5 = (bf16[1,10,2,64,512]{4,3,1,2,0:T(8,128)(2,1)S(1)}, bf16[1,10,2,64,512]{4,3,1,2,0:T(8,128)(2,1)S(1)}) fusion(s32[512]{0:T(512)S(1)} %iota_add_fusion.2, s32[10,2,64]{2,0,1:T(8,128)S(1)} %get-tuple-element.159, f32[10,2,64]{2,0,1:T(8,128)S(1)} %get-tuple-element.139, f32[10,2,64]{2,0,1:T(8,128)S(1)} %get-tuple-element.140), kind=kLoop, calls=%fused_computation.6.clone.1 | loop fusion | flops 8519680 | bytes 2638848 | tf_op jit(solution)/shard_map/convert
  95.2 0.6 fusion.42
  95.8 0.6 dynamic_slice.17
  97.1 11.9 %multiply_convert_fusion.5 = (bf16[1,10,2,64,512]{4,3,1,2,0:T(8,128)(2,1)S(1)}, bf16[1,10,2,64,512]{4,3,1,2,0:T(8,128)(2,1)S(1)}) fusion(s32[512]{0:T(512)S(1)} %iota_add_fusion.2, s32[10,2,64]{2,0,1:T(8,128)S(1)} %get-tuple-element.159, f32[10,2,64]{2,0,1:T(8,128)S(1)} %get-tuple-element.139, f32[10,2,64]{2,0,1:T(8,128)S(1)} %get-tuple-element.140), kind=kLoop, calls=%fused_computation.6.clone.1 | loop fusion | flops 8519680 | bytes 2638848 | tf_op jit(solution)/shard_map/convert
  109.0 0.6 fusion.42
  109.6 0.6 dynamic_slice.17
  110.8 11.9 %multiply_convert_fusion.5 = (bf16[1,10,2,64,512]{4,3,1,2,0:T(8,128)(2,1)S(1)}, bf16[1,10,2,64,512]{4,3,1,2,0:T(8,128)(2,1)S(1)}) fusion(s32[512]{0:T(512)S(1)} %iota_add_fusion.2, s32[10,2,64]{2,0,1:T(8,128)S(1)} %get-tuple-element.159, f32[10,2,64]{2,0,1:T(8,128)S(1)} %get-tuple-element.139, f32[10,2,64]{2,0,1:T(8,128)S(1)} %get-tuple-element.140), kind=kLoop, calls=%fused_computation.6.clone.1 | loop fusion | flops 8519680 | bytes 2638848 | tf_op jit(solution)/shard_map/convert
  122.8 0.6 fusion.42
  123.3 0.6 dynamic_slice.17
  124.6 11.9 %multiply_convert_fusion.5 = (bf16[1,10,2,64,512]{4,3,1,2,0:T(8,128)(2,1)S(1)}, bf16[1,10,2,64,512]{4,3,1,2,0:T(8,128)(2,1)S(1)}) fusion(s32[512]{0:T(512)S(1)} %iota_add_fusion.2, s32[10,2,64]{2,0,1:T(8,128)S(1)} %get-tuple-element.159, f32[10,2,64]{2,0,1:T(8,128)S(1)} %get-tuple-element.139, f32[10,2,64]{2,0,1:T(8,128)S(1)} %get-tuple-element.140), kind=kLoop, calls=%fused_computation.6.clone.1 | loop fusion | flops 8519680 | bytes 2638848 | tf_op jit(solution)/shard_map/convert
  136.5 0.6 fusion.42
  137.1 0.1 multiply_convert_fusion.2
  137.2 0.1 copy.49
  137.3 0.2 convert_element_type.82
  137.6 1.1 fusion.35
  138.7 244.8 %psum.14 = f32[16,256]{0,1:T(8,128)S(1)} all-reduce(f32[16,256]{0,1:T(8,128)S(1)} %fusion.35), channel_id=1, replica_groups=mesh['band'=64,'mem'=8] {'band'}, use_global_device_ids=true, to_apply=%region_3.4 | all-reduce | flops 4096 | bytes 32768 | tf_op jit(solution)/shard_map/psum | solution.py:95
  383.5 0.1 reshape.306
  383.6 0.1 copy.50
  383.7 14.0 %psum.15 = f32[8,4]{0,1:T(4,128)S(1)} all-reduce(f32[8,4]{0,1:T(4,128)S(1)} %reduce_sum.9), channel_id=1, replica_groups=mesh['band'=64,'mem'=8] {'mem'}, use_global_device_ids=true, to_apply=%region_5.6 | all-reduce | flops 32 | bytes 256 | tf_op jit(solution)/shard_map/psum | solution.py:100
  397.7 0.1 copy.51
  397.8 0.2 copy.48
  398.0 0.3 reshape.303
  398.3 0.8 multiply_convert_fusion.3
  399.1 0.6 broadcast_subtract_fusion
  (44 shorter events, 0.3 us)
Async XLA Ops:
  0.6 136.9 %copy-start = (bf16[2,2560,256]{2,1,0:T(8,128)(2,1)S(1)}, bf16[2,2560,256]{2,1,0:T(8,128)(2,1)}, u32[]{:S(2)}) copy-start(bf16[2,2560,256]{2,1,0:T(8,128)(2,1)} %param.11) | copy-start | bytes 7864324
  9.3 1.8 copy-start.1
  25.0 23.1 %copy-start.4 = (s32[10]{0:T(128)S(1)}, s32[10]{0:T(128)}, u32[]{:S(2)}) copy-start(s32[10]{0:T(128)} %param.9) | copy-start | bytes 124
  25.1 40.7 %copy-start.3 = (s32[64]{0:T(128)S(1)}, s32[64]{0:T(128)}, u32[]{:S(2)}) copy-start(s32[64]{0:T(128)} %param.10) | copy-start | bytes 772
  31.3 35.9 %all-to-all-start = ((bf16[64,2,640]{2,1,0:T(2,128)(2,1)}), bf16[64,2,640]{2,1,0:T(2,128)(2,1)S(1)}, u32[]{:S(2)}, u32[]{:S(2)}) async-start(bf16[64,2,640]{2,1,0:T(2,128)(2,1)} %broadcast_select_fusion), calls=%async_computation | async-start | bytes 327680 | tf_op jit(solution)/shard_map/all_to_all | solution.py:63
  68.3 13.2 %copy-start.2 = (bf16[64,2,10,2,2,4,2,2]{0,5,2,3,7,6,4,1:T(4,128)(2,1)S(1)}, bf16[64,2,10,2,2,4,2,2]{0,5,2,3,7,6,4,1:T(4,128)(2,1)}, u32[]{:S(2)}) copy-start(bf16[64,2,10,2,2,4,2,2]{0,5,2,3,7,6,4,1:T(4,128)(2,1)} %get-tuple-element.161) | copy-start | bytes 491524 | tf_op jit(solution)/shard_map/while
  82.0 13.2 %copy-start.2 = (bf16[64,2,10,2,2,4,2,2]{0,5,2,3,7,6,4,1:T(4,128)(2,1)S(1)}, bf16[64,2,10,2,2,4,2,2]{0,5,2,3,7,6,4,1:T(4,128)(2,1)}, u32[]{:S(2)}) copy-start(bf16[64,2,10,2,2,4,2,2]{0,5,2,3,7,6,4,1:T(4,128)(2,1)} %get-tuple-element.161) | copy-start | bytes 491524 | tf_op jit(solution)/shard_map/while
  95.8 13.2 %copy-start.2 = (bf16[64,2,10,2,2,4,2,2]{0,5,2,3,7,6,4,1:T(4,128)(2,1)S(1)}, bf16[64,2,10,2,2,4,2,2]{0,5,2,3,7,6,4,1:T(4,128)(2,1)}, u32[]{:S(2)}) copy-start(bf16[64,2,10,2,2,4,2,2]{0,5,2,3,7,6,4,1:T(4,128)(2,1)} %get-tuple-element.161) | copy-start | bytes 491524 | tf_op jit(solution)/shard_map/while
  109.6 13.2 %copy-start.2 = (bf16[64,2,10,2,2,4,2,2]{0,5,2,3,7,6,4,1:T(4,128)(2,1)S(1)}, bf16[64,2,10,2,2,4,2,2]{0,5,2,3,7,6,4,1:T(4,128)(2,1)}, u32[]{:S(2)}) copy-start(bf16[64,2,10,2,2,4,2,2]{0,5,2,3,7,6,4,1:T(4,128)(2,1)} %get-tuple-element.161) | copy-start | bytes 491524 | tf_op jit(solution)/shard_map/while
  123.3 13.2 %copy-start.2 = (bf16[64,2,10,2,2,4,2,2]{0,5,2,3,7,6,4,1:T(4,128)(2,1)S(1)}, bf16[64,2,10,2,2,4,2,2]{0,5,2,3,7,6,4,1:T(4,128)(2,1)}, u32[]{:S(2)}) copy-start(bf16[64,2,10,2,2,4,2,2]{0,5,2,3,7,6,4,1:T(4,128)(2,1)} %get-tuple-element.161) | copy-start | bytes 491524 | tf_op jit(solution)/shard_map/while
where the time goes:
time: 407 us; the launch traced here: 400 us
  blocking collectives  276 us (68%)
  other arithmetic  68.9 us (17%)
  local copies, waits for them, and re-layouts  23.8 us (6%)
  starting transfers between devices  14.8 us (4%)
  matrix products  11.2 us (3%)
    psum x1, blocking collectives, shards(): summed_all = lax.psum(partial_value, 'band')  245 us
    another operation x7, other arithmetic  59.7 us
    unnamed x1, blocking collectives  17 us
    all_to_all x1, starting transfers between devices, shards(): lax.all_to_all(packed, 'band', split_axis=0, concat_axis=0, tiled=True)  14.8 us
    psum x1, blocking collectives, shards(): summed = lax.psum(jnp.sum(local_share, axis=0), 'mem')  14 us
  transfers between devices with their start and end apart: 1, of which 0 were waited for; matrix products, arithmetic and copies ran while one was open for 1% of the time, Pallas kernels for 0%

commit v1 on v0

--- a/solution.py
+++ b/solution.py
@@ -92,12 +92,14 @@
         preferred_element_type=jnp.float32,
     )
     share_width = eof_modes // band_count
-    summed_all = lax.psum(partial_value, "band")
-    own_share = lax.dynamic_slice_in_dim(
-        summed_all, lax.axis_index("band") * share_width, share_width, 1
-    )
+    shares = partial_value.reshape(-1, band_count, share_width).transpose(1, 2, 0)
+    shares = lax.all_to_all(shares, "band", split_axis=0, concat_axis=0, tiled=True)
+    own_share = jnp.sum(shares, axis=0).T
     local_share = own_share.reshape(ens_dev, fields * level_stack, share_width)
-    summed = lax.psum(jnp.sum(local_share, axis=0), "mem")
+    local_sum = jnp.sum(local_share, axis=0)
+    member_groups = lax.axis_size("mem")
+    copies = jnp.broadcast_to(local_sum[None], (member_groups, *local_sum.shape))
+    summed = jnp.sum(lax.all_to_all(copies, "mem", 0, 0, tiled=True), axis=0)
     anomaly = local_share - summed / (ens_dev * lax.axis_size("mem"))
     return (grid_fields, anomaly.reshape(ens_dev, fields, level_stack, share_width))
 

time: 407 us -> 172 us (0.42); the launches traced: 400 us -> 171 us
  blocking collectives: 276 us -> 17 us
  starting transfers between devices: 14.8 us -> 31.2 us
  waiting for transfers between devices: 0.01 us -> 16.3 us
    psum x2 -> x0, blocking collectives: 259 us -> none  [the longest x1 245 us: shards(): summed_all = lax.psum(partial_value, 'band')]
    all_to_all x0 -> x2, starting transfers between devices: none -> 16.3 us  [the longest x1 9.53 us: shards(): lax.all_to_all(shares, 'band', split_axis=0, concat_axis=0, tiled=True)]
    all_to_all x0 -> x2, waiting for transfers between devices: none -> 16.3 us  [the longest x1 10.6 us: shards(): lax.all_to_all(shares, 'band', split_axis=0, concat_axis=0, tiled=True)]
  transfers between devices with their start and end apart: 1 -> 3, of which waited for: 0 -> 2; matrix products, arithmetic and copies ran while one was open for 1% -> 6% of each run, Pallas kernels for 0% -> 0%
where the time goes in v1:
time: 172 us; the launch traced here: 171 us
  other arithmetic  67.4 us (39%)
  starting transfers between devices  31.2 us (18%)
  local copies, waits for them, and re-layouts  24.3 us (14%)
  blocking collectives  17 us (10%)
  waiting for transfers between devices  16.3 us (9%)
  matrix products  9.97 us (6%)
  loops' own time  3.65 us (2%)
    another operation x7, other arithmetic  59.7 us
    unnamed x1, blocking collectives  17 us
    all_to_all x1, starting transfers between devices, shards(): lax.all_to_all(packed, 'band', split_axis=0, concat_axis=0, tiled=True)  14.8 us
    all_to_all x1, waiting for transfers between devices, shards(): lax.all_to_all(shares, 'band', split_axis=0, concat_axis=0, tiled=True)  10.6 us
    all_to_all x1, starting transfers between devices, shards(): lax.all_to_all(shares, 'band', split_axis=0, concat_axis=0, tiled=True)  9.53 us
    all_to_all x1, starting transfers between devices, shards(): summed = jnp.sum(lax.all_to_all(copies, 'mem', 0, 0, tiled=True), axis=0)  6.82 us
    all_to_all x1, waiting for transfers between devices, shards(): summed = jnp.sum(lax.all_to_all(copies, 'mem', 0, 0, tiled=True), axis=0)  5.7 us
    another operation x1, loops' own time, shards(): grid_parts = lax.map(synth_block, jnp.arange(lon_blocks, dtype=jnp.int32))  3.65 us
  transfers between devices with their start and end apart: 3, of which 2 were waited for; matrix products, arithmetic and copies ran while one was open for 6% of the time, Pallas kernels for 0%

profile of v1, /device:TPU:1, one launch (start us, length us, event | category | flops | bytes accessed | tf_op | source)
XLA Modules:
  0.0 171.5 jit_solution(18195041619951715504)
XLA Ops:
  0.7 0.7 broadcast_subtract_fusion.2
  1.5 0.7 copy.61
  2.2 0.1 reduce-window.9
  2.3 0.1 reduce
  2.4 0.7 sub.60
  3.1 1.7 %reshape.305 = bf16[32,10,11,128]{3,2,1,0:T(8,128)(2,1)S(1)} reshape(bf16[2,4,2,2,14080]{4,3,2,1,0:T(2,128)(2,1)} %param.7) | data formatting | bytes 1802240 | tf_op jit(solution)/shard_map/reshape | solution.py:30
  4.9 2.5 %reshape.309 = bf16[40,10,11,128]{3,2,1,0:T(8,128)(2,1)S(1)} reshape(bf16[40,14080]{1,0:T(8,128)(2,1)} %param.8) | data formatting | bytes 2252800 | tf_op jit(solution)/shard_map/reshape | solution.py:31
  7.3 0.1 fusion.31
  7.4 0.1 broadcast_multiply_fusion.1
  7.5 0.1 broadcast_multiply_fusion
  7.7 2.0 %fusion.22 = f32[10,11,32,40]{3,2,1,0:T(8,128)} fusion(bf16[40,10,11,128]{3,2,1,0:T(8,128)(2,1)S(1)} %reshape.309, bf16[32,10,11,128]{3,2,1,0:T(8,128)(2,1)S(1)} %broadcast_multiply_fusion.1), kind=kOutput, calls=%fused_computation.27 | convolution fusion | flops 36044800 | bytes 2590720 | tf_op jit(solution)/shard_map/cptk,jptk->ptcj/dot_general | solution.py:44
  9.7 0.8 fusion.20
  10.4 2.4 %rev.3 = f32[10,11,32,40]{3,2,1,0:T(8,128)} reverse(f32[10,11,32,40]{3,2,1,0:T(8,128)S(1)} %fusion.20), dimensions={3} | reverse | bytes 1126400 | tf_op jit(solution)/shard_map/rev | solution.py:53
  12.8 2.6 %pad_maximum_fusion = f32[10,11,32,80]{3,2,1,0:T(8,128)S(1)} fusion(f32[10,11,32,40]{3,2,1,0:T(8,128)} %rev.3, f32[10,11,32,40]{3,2,1,0:T(8,128)} %fusion.22), kind=kLoop, calls=%fused_computation.22 | loop fusion | flops 281600 | bytes 2252800 | tf_op jit(solution)/shard_map/concatenate | solution.py:53
  15.3 3.3 %fusion.17 = bf16[80,10,2,32]{0,2,3,1:T(2,128)(2,1)S(1)} fusion(f32[10,11,32,80]{3,2,1,0:T(8,128)S(1)} %pad_maximum_fusion, f32[10,1,11]{2,1,0:T(1,128)S(1)} %broadcast_subtract_fusion.1, f32[10,1,11]{2,1,0:T(1,128)S(1)} %compare_convert_fusion), kind=kOutput, calls=%fused_computation.24 | convolution fusion | flops 6809820 | bytes 1229680 | tf_op jit(solution)/shard_map/pht,ptcj->jphc/dot_general | solution.py:54
  18.6 0.4 copy.69
  19.1 0.1 copy.68
  19.2 0.1 min.22
  19.3 1.9 %gather_fusion = bf16[128,10,2,32]{3,2,1,0:T(2,128)(2,1)S(1)} fusion(bf16[80,10,2,32]{3,2,1,0:T(2,128)(2,1)S(1)} %copy.69, s32[1024]{0:T(1024)S(1)} %pad_clamp_fusion), kind=kCustom, calls=%fused_computation | custom fusion | bytes 328192 | tf_op jit(solution)/shard_map/jit(_take)/gather | solution.py:60
  21.3 0.7 gather.7
  22.0 0.1 copy.62
  22.1 0.9 broadcast_select_fusion
  23.0 14.8 %all-to-all-start = ((bf16[64,2,640]{2,1,0:T(2,128)(2,1)}), bf16[64,2,640]{2,1,0:T(2,128)(2,1)S(1)}, u32[]{:S(2)}, u32[]{:S(2)}) async-start(bf16[64,2,640]{2,1,0:T(2,128)(2,1)} %broadcast_select_fusion), calls=%async_computation | async-start | bytes 327680 | tf_op jit(solution)/shard_map/all_to_all | solution.py:63
  37.8 1.3 dynamic-slice
  39.9 0.2 dynamic-update-slice
  40.2 17.0 %all-reduce = s32[640]{0:T(1024)S(1)} all-reduce(s32[640]{0:T(1024)S(1)} %dynamic-update-slice), channel_id=1, replica_groups=mesh['band'=64,'mem'=8] {'band'}, use_global_device_ids=true, to_apply=%add | all-reduce | flops 640 | bytes 5120
  57.1 0.1 reshape.302
  57.5 0.6 dynamic_slice.10
  58.1 3.0 %copy.75 = bf16[5120,256]{0,1:T(8,128)(2,1)S(1)} copy(bf16[5120,256]{1,0:T(8,128)(2,1)} %bitcast.66) | data formatting | bytes 5242880 | tf_op jit(solution)/shard_map/reshape | solution.py:91
  61.1 2.4 %dot_general.26 = bf16[64,4,5120]{2,1,0:T(4,128)(2,1)} reshape(bf16[256,5120]{1,0:T(8,128)(2,1)S(1)} %bitcast.65) | data formatting | bytes 5242880 | tf_op jit(solution)/shard_map/dot_general | solution.py:89
  63.5 0.6 compare_convert_fusion.1
  64.2 0.3 copy.70
  64.4 0.1 copy.72
  64.6 68.9 %while.12 = (s32[]{:T(128)}, f32[5,2,4,2,2,512]{5,2,3,1,4,0:T(4,128)S(1)}, s32[10,2,64]{2,0,1:T(8,128)S(1)}, s32[5]{0:T(128)S(1)}, bf16[64,2,10,2,2,4,2,2]{0,5,2...) while((s32[]{:T(128)}, f32[5,2,4,2,2,512]{5,2,3,1,4,0:T(4,128)S(1)}, s32[10,2,64]{2,0,1:T(8,128)S(1)}, ...), condition=%wide.region_2.3_spmd, body=%wide.region_1.2_spmd.sunk | while | flops 97652992 | bytes 5671021 | solution.py:81
  64.6 0.6 dynamic_slice.12
  66.1 11.9 %multiply_convert_fusion.5 = (bf16[1,10,2,64,512]{4,3,1,2,0:T(8,128)(2,1)S(1)}, bf16[1,10,2,64,512]{4,3,1,2,0:T(8,128)(2,1)S(1)}) fusion(s32[512]{0:T(512)S(1)} %iota_add_fusion.2, s32[10,2,64]{2,0,1:T(8,128)S(1)} %get-tuple-element.164, f32[10,2,64]{2,0,1:T(8,128)S(1)} %get-tuple-element.144, f32[10,2,64]{2,0,1:T(8,128)S(1)} %get-tuple-element.145), kind=kLoop, calls=%fused_computation.6.clone.1 | loop fusion | flops 8519680 | bytes 2638848 | tf_op jit(solution)/shard_map/convert
  78.0 0.6 fusion.45
  78.5 0.6 dynamic_slice.12
  79.8 11.9 %multiply_convert_fusion.5 = (bf16[1,10,2,64,512]{4,3,1,2,0:T(8,128)(2,1)S(1)}, bf16[1,10,2,64,512]{4,3,1,2,0:T(8,128)(2,1)S(1)}) fusion(s32[512]{0:T(512)S(1)} %iota_add_fusion.2, s32[10,2,64]{2,0,1:T(8,128)S(1)} %get-tuple-element.164, f32[10,2,64]{2,0,1:T(8,128)S(1)} %get-tuple-element.144, f32[10,2,64]{2,0,1:T(8,128)S(1)} %get-tuple-element.145), kind=kLoop, calls=%fused_computation.6.clone.1 | loop fusion | flops 8519680 | bytes 2638848 | tf_op jit(solution)/shard_map/convert
  91.7 0.6 fusion.45
  92.3 0.6 dynamic_slice.12
  93.5 11.9 %multiply_convert_fusion.5 = (bf16[1,10,2,64,512]{4,3,1,2,0:T(8,128)(2,1)S(1)}, bf16[1,10,2,64,512]{4,3,1,2,0:T(8,128)(2,1)S(1)}) fusion(s32[512]{0:T(512)S(1)} %iota_add_fusion.2, s32[10,2,64]{2,0,1:T(8,128)S(1)} %get-tuple-element.164, f32[10,2,64]{2,0,1:T(8,128)S(1)} %get-tuple-element.144, f32[10,2,64]{2,0,1:T(8,128)S(1)} %get-tuple-element.145), kind=kLoop, calls=%fused_computation.6.clone.1 | loop fusion | flops 8519680 | bytes 2638848 | tf_op jit(solution)/shard_map/convert
  105.4 0.6 fusion.45
  106.0 0.6 dynamic_slice.12
  107.3 11.9 %multiply_convert_fusion.5 = (bf16[1,10,2,64,512]{4,3,1,2,0:T(8,128)(2,1)S(1)}, bf16[1,10,2,64,512]{4,3,1,2,0:T(8,128)(2,1)S(1)}) fusion(s32[512]{0:T(512)S(1)} %iota_add_fusion.2, s32[10,2,64]{2,0,1:T(8,128)S(1)} %get-tuple-element.164, f32[10,2,64]{2,0,1:T(8,128)S(1)} %get-tuple-element.144, f32[10,2,64]{2,0,1:T(8,128)S(1)} %get-tuple-element.145), kind=kLoop, calls=%fused_computation.6.clone.1 | loop fusion | flops 8519680 | bytes 2638848 | tf_op jit(solution)/shard_map/convert
  119.2 0.6 fusion.45
  119.8 0.6 dynamic_slice.12
  121.0 11.9 %multiply_convert_fusion.5 = (bf16[1,10,2,64,512]{4,3,1,2,0:T(8,128)(2,1)S(1)}, bf16[1,10,2,64,512]{4,3,1,2,0:T(8,128)(2,1)S(1)}) fusion(s32[512]{0:T(512)S(1)} %iota_add_fusion.2, s32[10,2,64]{2,0,1:T(8,128)S(1)} %get-tuple-element.164, f32[10,2,64]{2,0,1:T(8,128)S(1)} %get-tuple-element.144, f32[10,2,64]{2,0,1:T(8,128)S(1)} %get-tuple-element.145), kind=kLoop, calls=%fused_computation.6.clone.1 | loop fusion | flops 8519680 | bytes 2638848 | tf_op jit(solution)/shard_map/convert
  132.9 0.6 fusion.45
  133.5 0.1 multiply_convert_fusion.2
  133.6 0.1 copy.74
  133.7 0.2 reshape.331
  134.0 1.1 fusion.24
  135.1 0.8 copy.77
  135.9 9.5 %all-to-all-start.1 = ((f32[64,4,16]{2,1,0:T(4,128)}), f32[64,4,16]{2,1,0:T(4,128)S(1)}, u32[]{:S(2)}, u32[]{:S(2)}) async-start(f32[64,4,16]{2,1,0:T(4,128)} %copy.77), calls=%async_computation.1 | async-start | bytes 262144 | tf_op jit(solution)/shard_map/all_to_all | solution.py:96
  145.4 0.2 copy.73
  145.6 0.3 reshape.311
  145.9 10.6 %all-to-all-done.1 = f32[64,4,16]{2,1,0:T(4,128)S(1)} async-done(((f32[64,4,16]{2,1,0:T(4,128)}), f32[64,4,16]{2,1,0:T(4,128)S(1)}, u32[]{:S(2)}, u32[]{:S(2)}) %all-to-all-start.1) | async-done | bytes 16416 | tf_op jit(solution)/shard_map/all_to_all | solution.py:96
  156.6 0.1 reshape.314
  156.7 0.6 broadcast_in_dim.56
  157.3 6.8 %all-to-all-start.2 = ((f32[8,8,4]{1,2,0:T(4,128)}), f32[8,8,4]{1,2,0:T(4,128)S(1)}, u32[]{:S(2)}, u32[]{:S(2)}) async-start(f32[8,8,4]{1,2,0:T(4,128)} %broadcast_in_dim.56), calls=%async_computation.2 | async-start | bytes 32768 | tf_op jit(solution)/shard_map/all_to_all | solution.py:102
  164.1 0.8 multiply_convert_fusion.3
  165.1 5.7 %all-to-all-done.2 = f32[8,8,4]{1,2,0:T(4,128)S(1)} async-done(((f32[8,8,4]{1,2,0:T(4,128)}), f32[8,8,4]{1,2,0:T(4,128)S(1)}, u32[]{:S(2)}, u32[]{:S(2)}) %all-to-all-start.2) | async-done | bytes 1056 | tf_op jit(solution)/shard_map/all_to_all | solution.py:102
  170.9 0.6 broadcast_subtract_fusion
  (39 shorter events, 0.7 us)
Async XLA Ops:
  18.6 21.3 %copy-start.2 = (s32[10]{0:T(128)S(1)}, s32[10]{0:T(128)}, u32[]{:S(2)}) copy-start(s32[10]{0:T(128)} %param.9) | copy-start | bytes 124
  18.6 38.9 %copy-start.1 = (s32[64]{0:T(128)S(1)}, s32[64]{0:T(128)}, u32[]{:S(2)}) copy-start(s32[64]{0:T(128)} %param.10) | copy-start | bytes 772
  23.0 41.2 %all-to-all-start = ((bf16[64,2,640]{2,1,0:T(2,128)(2,1)}), bf16[64,2,640]{2,1,0:T(2,128)(2,1)S(1)}, u32[]{:S(2)}, u32[]{:S(2)}) async-start(bf16[64,2,640]{2,1,0:T(2,128)(2,1)} %broadcast_select_fusion), calls=%async_computation | async-start | bytes 327680 | tf_op jit(solution)/shard_map/all_to_all | solution.py:63
  64.6 69.4 %copy-start = (bf16[64,4,5120]{2,1,0:T(4,128)(2,1)S(1)}, bf16[64,4,5120]{2,1,0:T(4,128)(2,1)}, u32[]{:S(2)}) copy-start(bf16[64,4,5120]{2,1,0:T(4,128)(2,1)} %dot_general.26) | copy-start | bytes 7864324
  135.9 20.6 %all-to-all-start.1 = ((f32[64,4,16]{2,1,0:T(4,128)}), f32[64,4,16]{2,1,0:T(4,128)S(1)}, u32[]{:S(2)}, u32[]{:S(2)}) async-start(f32[64,4,16]{2,1,0:T(4,128)} %copy.77), calls=%async_computation.1 | async-start | bytes 262144 | tf_op jit(solution)/shard_map/all_to_all | solution.py:96
  157.3 13.4 %all-to-all-start.2 = ((f32[8,8,4]{1,2,0:T(4,128)}), f32[8,8,4]{1,2,0:T(4,128)S(1)}, u32[]{:S(2)}, u32[]{:S(2)}) async-start(f32[8,8,4]{1,2,0:T(4,128)} %broadcast_in_dim.56), calls=%async_computation.2 | async-start | bytes 32768 | tf_op jit(solution)/shard_map/all_to_all | solution.py:102

commit v2 on v0

v2 whole, which is shorter than its diff:
```python
import math

import jax
import jax.numpy as jnp
import numpy as np
from jax import lax
from jax.experimental import pallas as pl
from jax.experimental.pallas import tpu as pltpu
from jax.sharding import PartitionSpec as P

WAVE_COUNT = 1280
LON = 2560
BLK = 128
HALF = 40
BANDS = 64
PAIRS = 10
PAIR_LEN = 1408
FIELDS = 16
RADIX = 10
STEP = LON // RADIX
MODES = 256
SHARE = MODES // BANDS
SLOT_ROWS = 16
LOWS = WAVE_COUNT // 2
PER_CLASS = LOWS // RADIX
DIGIT = 16
KEEP_LANE = 2 * PAIRS
F32 = jnp.float32
BF16 = jnp.bfloat16


def wave_table():
    ladder = RADIX * np.arange(PER_CLASS)
    parts = []
    for c in range(RADIX):
        low = ladder + c
        high = WAVE_COUNT - RADIX - ladder + c
        orders = np.concatenate([low, high] if c % 2 == 0 else [high, low])
        phase = orders[:, None] * np.arange(STEP)[None, :] % LON
        angle = phase.astype(np.float32) * np.float32(2.0 * math.pi / LON)
        weight = np.where(orders == 0, 1.0, 2.0).astype(np.float32)[:, None]
        parts.append(np.concatenate([weight * np.cos(angle), -weight * np.sin(angle)]))
    return np.stack(parts).astype(jnp.bfloat16)


def legendre_kernel(
    waves, lengths, spectra_hbm, legendre_hbm, out, spectra_buf, legendre_buf, flat, sems
):
    def fetch(p):
        window = pl.ds(p * PAIR_LEN, PAIR_LEN)
        return (
            pltpu.make_async_copy(
                spectra_hbm.at[:, :, window], spectra_buf.at[p], sems.at[0, p]
            ),
            pltpu.make_async_copy(
                legendre_hbm.at[:, window], legendre_buf.at[p], sems.at[1, p]
            ),
        )

    for p in range(PAIRS):
        for copy in fetch(p):
            copy.start()
    counts = lengths[...].astype(F32)
    dest = lax.broadcasted_iota(jnp.int32, (BANDS, BANDS), 0)
    other = lax.broadcasted_iota(jnp.int32, (BANDS, BANDS), 1)
    starts = jnp.sum(jnp.where(other < dest, counts, 0.0), axis=1, keepdims=True)
    own = jnp.sum(jnp.where(other == dest, counts, 0.0), axis=1, keepdims=True)
    column = lax.broadcasted_iota(jnp.int32, (BANDS, 2 * HALF), 1).astype(F32)
    picks = []
    for r in range(2):
        row = jnp.minimum(starts + r, 2 * HALF - 1.0)
        source = jnp.where(row < HALF, row, 3 * HALF - 1.0 - row)
        picks.append((column == source).astype(BF16))
    pick = jnp.concatenate(picks, axis=0)
    lane = lax.broadcasted_iota(jnp.int32, (BANDS, BLK), 1)
    notes = jnp.where(lane == KEEP_LANE, jnp.where(own > 1.0, 1.0, 0.0), 0.0)
    position = lax.broadcasted_iota(jnp.int32, (FIELDS, PAIR_LEN), 1)
    parity = lax.broadcasted_iota(jnp.int32, (HALF, PAIR_LEN), 1) % 2
    alternate = jnp.where(parity == 0, 1.0, -1.0).astype(BF16)
    flat[...] = jnp.zeros(flat.shape, F32)
    for p in range(PAIRS):
        wave = waves[p]
        place = (wave % RADIX) * PER_CLASS + wave // RADIX
        notes = jnp.where(lane == p, (place // DIGIT).astype(F32), notes)
        notes = jnp.where(lane == PAIRS + p, (place % DIGIT).astype(F32), notes)
        upper = position - (WAVE_COUNT // BLK - wave // BLK) * BLK
        low = (position < WAVE_COUNT - wave).astype(F32).astype(BF16)
        high = ((upper >= 0) & (upper < wave + 1)).astype(F32).astype(BF16)
        for copy in fetch(p):
            copy.wait()
        coeffs = spectra_buf[p].reshape(2 * FIELDS, PAIR_LEN)
        halves = [jnp.concatenate([mask, mask], axis=0) * coeffs for mask in (low, high)]
        masked = jnp.concatenate(halves, axis=0)
        north = legendre_buf[p]
        rows = jnp.concatenate([north, north * alternate], axis=0)
        fourier = lax.dot_general(
            rows, masked, (((1,), (1,)), ((), ())), preferred_element_type=F32
        ).astype(BF16)
        picked = jnp.dot(pick, fourier, preferred_element_type=F32)
        flat[pl.ds(p, BANDS, stride=SLOT_ROWS), :] = jnp.concatenate(
            [picked[:BANDS], picked[BANDS:]], axis=1
        )
    flat[pl.ds(PAIRS, BANDS, stride=SLOT_ROWS), :] = notes
    out[...] = flat[...].astype(BF16).reshape(BANDS, SLOT_ROWS, BLK)


def synthesis_kernel(
    arrived, table_hbm, basis_hbm, grid_out, share_out,
    flat, sorted_buf, series, partial_buf, turned, table, basis, sems,
):
    table_copy = pltpu.make_async_copy(table_hbm, table, sems.at[0])
    basis_copy = pltpu.make_async_copy(basis_hbm, basis, sems.at[1])
    table_copy.start()
    basis_copy.start()
    flat[...] = arrived[...].reshape(BANDS * SLOT_ROWS, BLK).astype(F32)
    notes = flat[pl.ds(PAIRS, BANDS, stride=SLOT_ROWS), :]
    keep = notes[0:1, KEEP_LANE : KEEP_LANE + 1]
    target = lax.broadcasted_iota(jnp.int32, (BANDS, LOWS), 1).astype(F32)
    sources, hits = [], []
    for p in range(0, PAIRS, 2):
        couple = [flat[pl.ds(p + i, BANDS, stride=SLOT_ROWS), :] for i in range(2)]
        sources.append(jnp.concatenate(couple, axis=0).T.astype(BF16))
    for p in range(PAIRS):
        place = DIGIT * notes[:, p : p + 1] + notes[:, PAIRS + p : PAIRS + p + 1]
        hits.append(jnp.where(target == place, 1.0, 0.0).astype(BF16))
    by_wave = jnp.dot(
        jnp.concatenate(sources, axis=1),
        jnp.concatenate(hits, axis=0),
        preferred_element_type=F32,
    )
    for a in range(LOWS // BLK):
        sorted_buf[a] = by_wave[:, a * BLK : (a + 1) * BLK]
        for h in range(2):
            for c in range(2):
                for r in range(2):
                    series[2 * h + c, a, pl.ds(r, FIELDS, stride=2), :] = sorted_buf[
                        a, pl.ds(r * 64 + h * 32 + c, FIELDS, stride=2), :
                    ]
    first = lax.broadcasted_iota(jnp.int32, (2 * FIELDS, BLK), 1) < PER_CLASS
    table_copy.wait()
    real, imag = [], []
    for cls in range(RADIX):
        a = cls // 2
        b = RADIX // 2 - 1 - a
        halves = []
        for c in range(2):
            low = series[c, a]
            high = series[2 + c, b]
            halves.append(jnp.where(first, low, high) if cls % 2 == 0 else jnp.where(first, high, low))
        re, im = halves
        lhs = jnp.concatenate(
            [jnp.concatenate([re, im], axis=1), jnp.concatenate([im, -re], axis=1)], axis=0
        ).astype(BF16)
        both = jnp.dot(lhs, table[cls], preferred_element_type=F32)
        real.append(both[: 2 * FIELDS])
        imag.append(both[2 * FIELDS :])
    pieces = [None] * RADIX
    for q in range(3):
        sums = []
        for part, wave in ((real, math.cos), (imag, math.sin)):
            for odd in range(2):
                total = None
                for cls in range(odd, RADIX, 2):
                    factor = wave(2.0 * math.pi * cls * q / RADIX)
                    if abs(factor) < 1e-9:
                        continue
                    term = part[cls] if factor == 1.0 else part[cls] * factor
                    total = term if total is None else total + term
                sums.append(total)
        cos_even, cos_odd, sin_even, sin_odd = sums
        if q == 0:
            pieces[0] = cos_even + cos_odd
            pieces[5] = cos_even - cos_odd
        else:
            pieces[q] = (cos_even + cos_odd) - (sin_even + sin_odd)
            pieces[10 - q] = (cos_even + cos_odd) + (sin_even + sin_odd)
            pieces[5 - q] = (cos_even - cos_odd) + (sin_even - sin_odd)
            pieces[5 + q] = (cos_even - cos_odd) - (sin_even - sin_odd)
    second = lax.broadcasted_iota(jnp.int32, (2 * FIELDS, STEP), 0) % 2
    kept = keep > 0.5
    basis_copy.wait()
    total = jnp.zeros((2 * FIELDS, MODES), F32)
    for q in range(RADIX):
        window = slice(q * STEP, (q + 1) * STEP)
        upper_row = jnp.where(second == 0, pieces[q], 0.0)
        lower_row = jnp.where((second == 1) & kept, pieces[q], 0.0)
        grid_out[:, :, window] = (
            (upper_row + lower_row).astype(BF16).reshape(FIELDS, 2, STEP)
        )
        total += jnp.dot(upper_row.astype(BF16), basis[0, window, :], preferred_element_type=F32)
        total += jnp.dot(lower_row.astype(BF16), basis[1, window, :], preferred_element_type=F32)
    for i in range(MODES // BLK):
        partial_buf[i] = total[:, i * BLK : (i + 1) * BLK]
        turned[i * BLK : (i + 1) * BLK, :FIELDS] = (
            partial_buf[i, pl.ds(0, FIELDS, stride=2), :]
            + partial_buf[i, pl.ds(1, FIELDS, stride=2), :]
        ).T
    share_out[...] = jnp.concatenate(
        [turned[pl.ds(o, BANDS, stride=SHARE), :][:, :FIELDS] for o in range(SHARE)], axis=1
    )


def sum_kernel(shares, out):
    out[...] = jnp.broadcast_to(jnp.sum(shares[...], axis=0, keepdims=True), out.shape)


VMEM = pl.BlockSpec(memory_space=pltpu.VMEM)
SMEM = pl.BlockSpec(memory_space=pltpu.SMEM)
HBM = pl.BlockSpec(memory_space=pl.ANY)
PARAMS = pltpu.CompilerParams(vmem_limit_bytes=48 * 1024 * 1024)


def to_messages(waves, lengths, spectra, legendre):
    return pl.pallas_call(
        legendre_kernel,
        out_shape=jax.ShapeDtypeStruct((BANDS, SLOT_ROWS, BLK), BF16),
        in_specs=[SMEM, VMEM, HBM, HBM],
        out_specs=VMEM,
        scratch_shapes=[
            pltpu.VMEM((PAIRS, FIELDS, 2, PAIR_LEN), BF16),
            pltpu.VMEM((PAIRS, HALF, PAIR_LEN), BF16),
            pltpu.VMEM((BANDS * SLOT_ROWS, BLK), F32),
            pltpu.SemaphoreType.DMA((2, PAIRS)),
        ],
        compiler_params=PARAMS,
    )(waves, lengths, spectra, legendre)


def to_grid(arrived, table, basis):
    return pl.pallas_call(
        synthesis_kernel,
        out_shape=(
            jax.ShapeDtypeStruct((FIELDS, 2, LON), BF16),
            jax.ShapeDtypeStruct((BANDS, SHARE * FIELDS), F32),
        ),
        in_specs=[VMEM, HBM, HBM],
        out_specs=(VMEM, VMEM),
        scratch_shapes=[
            pltpu.VMEM((BANDS * SLOT_ROWS, BLK), F32),
            pltpu.VMEM((LOWS // BLK, BLK, BLK), F32),
            pltpu.VMEM((4, LOWS // BLK, 2 * FIELDS, BLK), F32),
            pltpu.VMEM((MODES // BLK, 2 * FIELDS, BLK), F32),
            pltpu.VMEM((MODES, BLK), F32),
            pltpu.VMEM((RADIX, STEP, STEP), BF16),
            pltpu.VMEM((2, LON, MODES), BF16),
            pltpu.SemaphoreType.DMA((2,)),
        ],
        compiler_params=PARAMS,
    )(arrived, table, basis)


def to_sums(shares, copies):
    return pl.pallas_call(
        sum_kernel,
        out_shape=jax.ShapeDtypeStruct((copies, SHARE * FIELDS), F32),
        in_specs=[VMEM],
        out_specs=VMEM,
    )(shares)


def shards(spectra, legendre, pair_waves, band_lengths, eof_basis):
    ens, fields, levels, parts, slots = spectra.shape
    messages = to_messages(
        pair_waves,
        band_lengths.reshape(1, BANDS),
        spectra.reshape(FIELDS, parts, slots),
        legendre,
    )
    arrived = lax.all_to_all(messages, "band", 0, 0, tiled=True)
    grid, shares = to_grid(arrived, jnp.asarray(wave_table()), eof_basis)
    shares = lax.all_to_all(shares, "band", 0, 0, tiled=True)
    groups = lax.axis_size("mem")
    sums = to_sums(shares, groups)
    everyone = lax.all_to_all(sums, "mem", 0, 0, tiled=True)
    own = sums[0].reshape(SHARE, ens, fields * levels)
    total = jnp.sum(everyone, axis=0).reshape(SHARE, ens, fields * levels)
    mean = jnp.sum(total, axis=1, keepdims=True) / (ens * groups)
    anomaly = (own - mean).transpose(1, 2, 0).reshape(ens, fields, levels, SHARE)
    return grid.reshape(ens, fields, levels, 2, LON), anomaly


def solution(mesh):
    return jax.shard_map(
        shards,
        mesh=mesh,
        in_specs=(
            P("mem", None, None, None, "band"),
            P(None, "band"),
            P("band"),
            P(),
            P("band", None, None),
        ),
        out_specs=(P("mem", None, None, "band", None), P("mem", None, None, "band")),
        check_vma=False,
    )
```

time: 407 us -> 72 us (0.18); the launches traced: 400 us -> 71.6 us
  blocking collectives: 276 us -> 41.9 us
  other arithmetic: 68.9 us -> 0.06 us
  local copies, waits for them, and re-layouts: 23.8 us -> 6.65 us
  matrix products: 11.2 us -> 0 us
  Pallas kernels: 0 us -> 9.86 us
  starting transfers between devices: 14.8 us -> 6.82 us
  waiting for transfers between devices: 0.01 us -> 5.63 us
    psum x2 -> x0, blocking collectives: 259 us -> none  [the longest x1 245 us: shards(): summed_all = lax.psum(partial_value, 'band')]
    another operation x9 -> x0, other arithmetic: 59.7 us -> none
    all_to_all x0 -> x2, blocking collectives: none -> 41.9 us  [the longest x1 27.8 us: shards(): arrived = lax.all_to_all(messages, 'band', 0, 0, tiled=True)]
    unnamed x1 -> x0, blocking collectives: 17 us -> none
    dot_general x9 -> x0, matrix products: 11.2 us -> none  [the longest x1 3.26 us: shards(): jnp.einsum('pht,ptcj->jphc', owners, rows_all, precision=lax.Precision.HI...]
    pallas_call x0 -> x3, Pallas kernels: none -> 9.86 us  [the longest x1 6.02 us: to_messages(): pl.pallas_call(legendre_kernel, out_shape=jax.ShapeDtypeStruct((BANDS, SL...]
    all_to_all x1, starting transfers between devices: 14.8 us -> 6.82 us  [shards(): everyone = lax.all_to_all(sums, 'mem', 0, 0, tiled=True)]
    reshape x5 -> x1, local copies, waits for them, and re-layouts: 6.47 us -> 0.09 us  [shards(): total = jnp.sum(everyone, axis=0).reshape(SHARE, ens, fields * levels)]
  transfers between devices with their start and end apart: 1 -> 1, of which waited for: 0 -> 1; matrix products, arithmetic and copies ran while one was open for 1% -> 1% of each run, Pallas kernels for 0% -> 0%
where the time goes in v2:
time: 72 us; the launch traced here: 71.6 us
  blocking collectives  41.9 us (58%)
  Pallas kernels  9.86 us (14%)
  starting transfers between devices  6.82 us (9%)
  local copies, waits for them, and re-layouts  6.65 us (9%)
  waiting for transfers between devices  5.63 us (8%)
    all_to_all x1, blocking collectives, shards(): arrived = lax.all_to_all(messages, 'band', 0, 0, tiled=True)  27.8 us
    all_to_all x1, blocking collectives, shards(): shares = lax.all_to_all(shares, 'band', 0, 0, tiled=True)  14.1 us
    all_to_all x1, starting transfers between devices, shards(): everyone = lax.all_to_all(sums, 'mem', 0, 0, tiled=True)  6.82 us
    pallas_call x1, Pallas kernels, to_messages(): pl.pallas_call(legendre_kernel, out_shape=jax.ShapeDtypeStruct((BANDS, SL...  6.02 us
    all_to_all x1, waiting for transfers between devices, shards(): everyone = lax.all_to_all(sums, 'mem', 0, 0, tiled=True)  5.63 us
    unnamed x12, local copies, waits for them, and re-layouts  5.05 us
    pallas_call x1, Pallas kernels, to_grid(): pl.pallas_call(synthesis_kernel, out_shape=(jax.ShapeDtypeStruct((FIELDS,...  2.47 us
  transfers between devices with their start and end apart: 1, of which 1 were waited for; matrix products, arithmetic and copies ran while one was open for 1% of the time, Pallas kernels for 0%

profile of v2, /device:TPU:1, one launch (start us, length us, event | category | flops | bytes accessed | tf_op | source)
XLA Modules:
  0.0 71.6 jit_solution(15823746695175176667)
XLA Ops:
  0.6 0.0 copy-start.2
  0.6 1.2 %copy-done.2 = bf16[40,14080]{1,0:T(8,128)(2,1)S(1)} copy-done((bf16[40,14080]{1,0:T(8,128)(2,1)S(1)}, bf16[40,14080]{1,0:T(8,128)(2,1)}, u32[]{:S(2)}) %copy-start.2) | copy-done | bytes 1126424
  1.9 0.0 copy-start.3
  1.9 1.2 %copy-done.3 = bf16[2,4,2,2,14080]{4,3,2,1,0:T(2,128)(2,1)S(1)} copy-done((bf16[2,4,2,2,14080]{4,3,2,1,0:T(2,128)(2,1)S(1)}, bf16[2,4,2,2,14080]{4,3,2,1,0:T(2,128)(2,1)}, u32[]{:S(2)}) %copy-start.3) | copy-done | bytes 901144
  3.1 0.0 copy-start.4
  3.1 0.7 copy-done.4
  3.7 0.0 copy-start.5
  3.7 0.7 copy-done.5
  4.4 0.0 copy-start
  4.4 6.0 %shard_map.77 = bf16[64,16,128]{2,1,0:T(8,128)(2,1)S(1)} custom-call(s32[10]{0:T(128)S(1)} %copy-done.4, s32[1,64]{1,0:T(1,128)S(1)} %bitcast.15, bf16[16,2,14080]{2,1,0:T(2,128)(2,1)S(1)} %bitcast.13, bf16[40,14080]{1,0:T(8,128)(2,1)S(1)} %copy-done.2), custom_call_target="tpu_custom_call" | custom-call | tf_op jit(solution)/shard_map/pallas_call | solution.py:214
  10.4 27.8 %all_to_all.25.arrived = bf16[64,16,128]{2,1,0:T(8,128)(2,1)S(1)} all-to-all(bf16[64,16,128]{2,1,0:T(8,128)(2,1)S(1)} %shard_map.77), channel_id=1, replica_groups=mesh['band'=64,'mem'=8] {'band'}, dimensions={0} | all-to-all | bytes 524288 | tf_op jit(solution)/shard_map/all_to_all | solution.py:269
  38.2 0.0 copy-done
  38.2 0.0 copy-start.1
  38.2 1.3 %copy-done.1 = bf16[10,256,256]{2,1,0:T(8,128)(2,1)S(1)} copy-done((bf16[10,256,256]{2,1,0:T(8,128)(2,1)S(1)}, bf16[10,256,256]{2,1,0:T(8,128)(2,1)}, u32[]{:S(2)}) %copy-start.1) | copy-done | bytes 1310744
  39.5 2.5 %shard_map.78 = (bf16[16,2,2560]{2,1,0:T(2,128)(2,1)}, f32[64,64]{1,0:T(8,128)S(1)}) custom-call(bf16[64,16,128]{2,1,0:T(8,128)(2,1)S(1)} %all_to_all.25.arrived, bf16[10,256,256]{2,1,0:T(8,128)(2,1)S(1)} %copy-done.1, bf16[2,2560,256]{2,1,0:T(8,128)(2,1)S(1)} %copy-done), custom_call_target="tpu_custom_call" | custom-call | tf_op jit(solution)/shard_map/pallas_call | solution.py:230
  42.0 14.1 %all_to_all.26 = f32[64,1,64]{2,1,0:T(1,128)} all-to-all(f32[64,1,64]{2,1,0:T(1,128)S(1)} %bitcast.14), channel_id=1, replica_groups=mesh['band'=64,'mem'=8] {'band'}, dimensions={0} | all-to-all | bytes 32768 | tf_op jit(solution)/shard_map/all_to_all | solution.py:271
  56.1 1.4 %shard_map.79 = f32[8,64]{1,0:T(8,128)} custom-call(f32[64,64]{1,0:T(8,128)} %bitcast.16), custom_call_target="tpu_custom_call" | custom-call | tf_op jit(solution)/shard_map/pallas_call | solution.py:253
  57.5 6.8 %all-to-all-start.2 = ((f32[8,1,64]{2,1,0:T(1,128)}), f32[8,1,64]{2,1,0:T(1,128)S(1)}, u32[]{:S(2)}, u32[]{:S(2)}) async-start(f32[8,1,64]{2,1,0:T(1,128)} %bitcast.17), calls=%async_computation.2 | async-start | bytes 8192 | tf_op jit(solution)/shard_map/all_to_all | solution.py:274
  64.3 0.7 %slice_reduce_fusion = f32[64]{0:T(128)S(1)} fusion(f32[8,64]{1,0:T(8,128)} %shard_map.79), kind=kLoop, calls=%fused_computation.2 | loop fusion | bytes 512 | tf_op jit(solution)/shard_map/slice | solution.py:275
  65.0 0.1 reshape_squeeze.3
  65.1 5.6 %all-to-all-done.2 = f32[8,1,64]{2,1,0:T(1,128)S(1)} async-done(((f32[8,1,64]{2,1,0:T(1,128)}), f32[8,1,64]{2,1,0:T(1,128)S(1)}, u32[]{:S(2)}, u32[]{:S(2)}) %all-to-all-start.2) | async-done | bytes 2080 | tf_op jit(solution)/shard_map/all_to_all | solution.py:274
  70.8 0.1 reshape.30
  70.9 0.7 copy.11
  (4 shorter events, 0.1 us)
Async XLA Ops:
  0.6 1.3 %copy-start.2 = (bf16[40,14080]{1,0:T(8,128)(2,1)S(1)}, bf16[40,14080]{1,0:T(8,128)(2,1)}, u32[]{:S(2)}) copy-start(bf16[40,14080]{1,0:T(8,128)(2,1)} %legendre_hbm.1) | copy-start | bytes 3379204
  1.9 1.2 %copy-start.3 = (bf16[2,4,2,2,14080]{4,3,2,1,0:T(2,128)(2,1)S(1)}, bf16[2,4,2,2,14080]{4,3,2,1,0:T(2,128)(2,1)}, u32[]{:S(2)}) copy-start(bf16[2,4,2,2,14080]{4,3,2,1,0:T(2,128)(2,1)} %param.6) | copy-start | bytes 2703364
  3.1 0.7 copy-start.4
  3.7 0.7 copy-start.5
  4.4 33.8 %copy-start = (bf16[2,2560,256]{2,1,0:T(8,128)(2,1)S(1)}, bf16[2,2560,256]{2,1,0:T(8,128)(2,1)}, u32[]{:S(2)}) copy-start(bf16[2,2560,256]{2,1,0:T(8,128)(2,1)} %basis_hbm.1) | copy-start | bytes 7864324
  38.2 1.3 %copy-start.1 = (bf16[10,256,256]{2,1,0:T(8,128)(2,1)S(1)}, bf16[10,256,256]{2,1,0:T(8,128)(2,1)}, u32[]{:S(2)}) copy-start(bf16[10,256,256]{2,1,0:T(8,128)(2,1)} %constant.7.clone.table_hbm) | copy-start | bytes 3932164
  57.5 13.3 %all-to-all-start.2 = ((f32[8,1,64]{2,1,0:T(1,128)}), f32[8,1,64]{2,1,0:T(1,128)S(1)}, u32[]{:S(2)}, u32[]{:S(2)}) async-start(f32[8,1,64]{2,1,0:T(1,128)} %bitcast.17), calls=%async_computation.2 | async-start | bytes 8192 | tf_op jit(solution)/shard_map/all_to_all | solution.py:274

commit v3 on v2

--- a/solution.py
+++ b/solution.py
@@ -20,7 +20,8 @@
 STEP = LON // RADIX
 MODES = 256
 SHARE = MODES // BANDS
-SLOT_ROWS = 16
+SLOT_ROWS = 12
+LOADS = 2
 LOWS = WAVE_COUNT // 2
 PER_CLASS = LOWS // RADIX
 DIGIT = 16
@@ -44,22 +45,29 @@
 
 
 def legendre_kernel(
-    waves, lengths, spectra_hbm, legendre_hbm, out, spectra_buf, legendre_buf, flat, sems
+    waves_hbm, lengths_hbm, spectra_hbm, legendre_hbm, out,
+    waves, lengths, spectra_buf, legendre_buf, flat, sems, small_sems,
 ):
-    def fetch(p):
-        window = pl.ds(p * PAIR_LEN, PAIR_LEN)
-        return (
+    waves_copy = pltpu.make_async_copy(waves_hbm, waves, small_sems.at[0])
+    lengths_copy = pltpu.make_async_copy(lengths_hbm, lengths, small_sems.at[1])
+    waves_copy.start()
+    lengths_copy.start()
+
+    loads = []
+    for i in range(LOADS):
+        window = pl.ds(i * (PAIRS // LOADS) * PAIR_LEN, (PAIRS // LOADS) * PAIR_LEN)
+        loads += [
             pltpu.make_async_copy(
-                spectra_hbm.at[:, :, window], spectra_buf.at[p], sems.at[0, p]
+                spectra_hbm.at[:, :, window], spectra_buf.at[:, :, window], sems.at[0, i]
             ),
             pltpu.make_async_copy(
-                legendre_hbm.at[:, window], legendre_buf.at[p], sems.at[1, p]
+                legendre_hbm.at[:, window], legendre_buf.at[:, window], sems.at[1, i]
             ),
-        )
-
-    for p in range(PAIRS):
-        for copy in fetch(p):
-            copy.start()
+        ]
+    for load in loads:
+        load.start()
+    waves_copy.wait()
+    lengths_copy.wait()
     counts = lengths[...].astype(F32)
     dest = lax.broadcasted_iota(jnp.int32, (BANDS, BANDS), 0)
     other = lax.broadcasted_iota(jnp.int32, (BANDS, BANDS), 1)
@@ -78,6 +86,9 @@
     parity = lax.broadcasted_iota(jnp.int32, (HALF, PAIR_LEN), 1) % 2
     alternate = jnp.where(parity == 0, 1.0, -1.0).astype(BF16)
     flat[...] = jnp.zeros(flat.shape, F32)
+    for load in loads:
+        load.wait()
+    half = BLK // 2
     for p in range(PAIRS):
         wave = waves[p]
         place = (wave % RADIX) * PER_CLASS + wave // RADIX
@@ -86,33 +97,44 @@
         upper = position - (WAVE_COUNT // BLK - wave // BLK) * BLK
         low = (position < WAVE_COUNT - wave).astype(F32).astype(BF16)
         high = ((upper >= 0) & (upper < wave + 1)).astype(F32).astype(BF16)
-        for copy in fetch(p):
-            copy.wait()
-        coeffs = spectra_buf[p].reshape(2 * FIELDS, PAIR_LEN)
+        window = slice(p * PAIR_LEN, (p + 1) * PAIR_LEN)
+        coeffs = spectra_buf[:, :, window].reshape(2 * FIELDS, PAIR_LEN)
         halves = [jnp.concatenate([mask, mask], axis=0) * coeffs for mask in (low, high)]
         masked = jnp.concatenate(halves, axis=0)
-        north = legendre_buf[p]
+        north = legendre_buf[:, window]
         rows = jnp.concatenate([north, north * alternate], axis=0)
         fourier = lax.dot_general(
             rows, masked, (((1,), (1,)), ((), ())), preferred_element_type=F32
-        ).astype(BF16)
-        picked = jnp.dot(pick, fourier, preferred_element_type=F32)
+        )
+        if p % 2 == 0:
+            first = fourier
+            continue
+        couple = jnp.concatenate([first, fourier], axis=1).astype(BF16)
+        picked = jnp.dot(pick, couple, preferred_element_type=F32)
+        top, bottom = picked[:BANDS], picked[BANDS:]
+        flat[pl.ds(p - 1, BANDS, stride=SLOT_ROWS), :] = jnp.concatenate(
+            [top[:, :half], bottom[:, :half]], axis=1
+        )
         flat[pl.ds(p, BANDS, stride=SLOT_ROWS), :] = jnp.concatenate(
-            [picked[:BANDS], picked[BANDS:]], axis=1
+            [top[:, half:], bottom[:, half:]], axis=1
         )
     flat[pl.ds(PAIRS, BANDS, stride=SLOT_ROWS), :] = notes
-    out[...] = flat[...].astype(BF16).reshape(BANDS, SLOT_ROWS, BLK)
+    out[...] = flat[...].astype(BF16)
 
 
 def synthesis_kernel(
-    arrived, table_hbm, basis_hbm, grid_out, share_out,
-    flat, sorted_buf, series, partial_buf, turned, table, basis, sems,
+    arrived, table_hbm, basis, grid_out, share_out,
+    flat, sorted_buf, series, partial_buf, turned, table, sems,
 ):
-    table_copy = pltpu.make_async_copy(table_hbm, table, sems.at[0])
-    basis_copy = pltpu.make_async_copy(basis_hbm, basis, sems.at[1])
-    table_copy.start()
-    basis_copy.start()
-    flat[...] = arrived[...].reshape(BANDS * SLOT_ROWS, BLK).astype(F32)
+    loads = [
+        pltpu.make_async_copy(
+            table_hbm.at[pl.ds(i, 2)], table.at[pl.ds(i, 2)], sems.at[i // 2]
+        )
+        for i in range(0, RADIX, 2)
+    ]
+    for load in loads:
+        load.start()
+    flat[...] = arrived[...].astype(F32)
     notes = flat[pl.ds(PAIRS, BANDS, stride=SLOT_ROWS), :]
     keep = notes[0:1, KEEP_LANE : KEEP_LANE + 1]
     target = lax.broadcasted_iota(jnp.int32, (BANDS, LOWS), 1).astype(F32)
@@ -137,7 +159,8 @@
                         a, pl.ds(r * 64 + h * 32 + c, FIELDS, stride=2), :
                     ]
     first = lax.broadcasted_iota(jnp.int32, (2 * FIELDS, BLK), 1) < PER_CLASS
-    table_copy.wait()
+    for load in loads:
+        load.wait()
     real, imag = [], []
     for cls in range(RADIX):
         a = cls // 2
@@ -178,7 +201,6 @@
             pieces[5 + q] = (cos_even - cos_odd) - (sin_even - sin_odd)
     second = lax.broadcasted_iota(jnp.int32, (2 * FIELDS, STEP), 0) % 2
     kept = keep > 0.5
-    basis_copy.wait()
     total = jnp.zeros((2 * FIELDS, MODES), F32)
     for q in range(RADIX):
         window = slice(q * STEP, (q + 1) * STEP)
@@ -200,30 +222,28 @@
     )
 
 
-def sum_kernel(shares, out):
-    out[...] = jnp.broadcast_to(jnp.sum(shares[...], axis=0, keepdims=True), out.shape)
-
-
 VMEM = pl.BlockSpec(memory_space=pltpu.VMEM)
-SMEM = pl.BlockSpec(memory_space=pltpu.SMEM)
-HBM = pl.BlockSpec(memory_space=pl.ANY)
+HBM = pl.BlockSpec(memory_space=pltpu.HBM)
 PARAMS = pltpu.CompilerParams(vmem_limit_bytes=48 * 1024 * 1024)
 
 
 def to_messages(waves, lengths, spectra, legendre):
     return pl.pallas_call(
         legendre_kernel,
-        out_shape=jax.ShapeDtypeStruct((BANDS, SLOT_ROWS, BLK), BF16),
-        in_specs=[SMEM, VMEM, HBM, HBM],
+        out_shape=jax.ShapeDtypeStruct((BANDS * SLOT_ROWS, BLK), BF16),
+        in_specs=[HBM, HBM, HBM, HBM],
         out_specs=VMEM,
         scratch_shapes=[
-            pltpu.VMEM((PAIRS, FIELDS, 2, PAIR_LEN), BF16),
-            pltpu.VMEM((PAIRS, HALF, PAIR_LEN), BF16),
+            pltpu.SMEM((PAIRS,), jnp.int32),
+            pltpu.VMEM((1, BANDS), jnp.int32),
+            pltpu.VMEM((FIELDS, 2, PAIRS * PAIR_LEN), BF16),
+            pltpu.VMEM((HALF, PAIRS * PAIR_LEN), BF16),
             pltpu.VMEM((BANDS * SLOT_ROWS, BLK), F32),
-            pltpu.SemaphoreType.DMA((2, PAIRS)),
+            pltpu.SemaphoreType.DMA((2, LOADS)),
+            pltpu.SemaphoreType.DMA((2,)),
         ],
         compiler_params=PARAMS,
-    )(waves, lengths, spectra, legendre)
+    )(*[pltpu.with_memory_space_constraint(x, pltpu.HBM) for x in (waves, lengths, spectra, legendre)])
 
 
 def to_grid(arrived, table, basis):
@@ -233,7 +253,7 @@
             jax.ShapeDtypeStruct((FIELDS, 2, LON), BF16),
             jax.ShapeDtypeStruct((BANDS, SHARE * FIELDS), F32),
         ),
-        in_specs=[VMEM, HBM, HBM],
+        in_specs=[VMEM, HBM, VMEM],
         out_specs=(VMEM, VMEM),
         scratch_shapes=[
             pltpu.VMEM((BANDS * SLOT_ROWS, BLK), F32),
@@ -242,20 +262,10 @@
             pltpu.VMEM((MODES // BLK, 2 * FIELDS, BLK), F32),
             pltpu.VMEM((MODES, BLK), F32),
             pltpu.VMEM((RADIX, STEP, STEP), BF16),
-            pltpu.VMEM((2, LON, MODES), BF16),
-            pltpu.SemaphoreType.DMA((2,)),
+            pltpu.SemaphoreType.DMA((RADIX // 2,)),
         ],
         compiler_params=PARAMS,
-    )(arrived, table, basis)
-
-
-def to_sums(shares, copies):
-    return pl.pallas_call(
-        sum_kernel,
-        out_shape=jax.ShapeDtypeStruct((copies, SHARE * FIELDS), F32),
-        in_specs=[VMEM],
-        out_specs=VMEM,
-    )(shares)
+    )(arrived, pltpu.with_memory_space_constraint(table, pltpu.HBM), basis)
 
 
 def shards(spectra, legendre, pair_waves, band_lengths, eof_basis):
@@ -266,11 +276,13 @@
         spectra.reshape(FIELDS, parts, slots),
         legendre,
     )
+    messages = messages.reshape(BANDS, SLOT_ROWS // 2, 2, BLK)
     arrived = lax.all_to_all(messages, "band", 0, 0, tiled=True)
+    arrived = arrived.reshape(BANDS * SLOT_ROWS, BLK)
     grid, shares = to_grid(arrived, jnp.asarray(wave_table()), eof_basis)
     shares = lax.all_to_all(shares, "band", 0, 0, tiled=True)
     groups = lax.axis_size("mem")
-    sums = to_sums(shares, groups)
+    sums = jnp.broadcast_to(jnp.sum(shares, axis=0)[None], (groups, SHARE * FIELDS))
     everyone = lax.all_to_all(sums, "mem", 0, 0, tiled=True)
     own = sums[0].reshape(SHARE, ens, fields * levels)
     total = jnp.sum(everyone, axis=0).reshape(SHARE, ens, fields * levels)

time: 72 us -> 62.5 us (0.87)
  local copies, waits for them, and re-layouts: 6.65 us -> 1.46 us
  Pallas kernels: 9.86 us -> 6.46 us
  blocking collectives: 41.9 us -> 40.3 us
  waiting for transfers between devices: 5.63 us -> 6.37 us
    unnamed x12 -> x2, local copies, waits for them, and re-layouts: 5.05 us -> 0.01 us
    pallas_call x2 -> x1, Pallas kernels: 7.39 us -> 3.64 us  [to_messages(): pl.pallas_call(legendre_kernel, out_shape=jax.ShapeDtypeStruct((BANDS * S...]
    all_to_all x1, blocking collectives: 27.8 us -> 26.7 us  [shards(): arrived = lax.all_to_all(messages, 'band', 0, 0, tiled=True)]
    all_to_all x1, waiting for transfers between devices: 5.63 us -> 6.37 us  [shards(): everyone = lax.all_to_all(sums, 'mem', 0, 0, tiled=True)]
  transfers between devices with their start and end apart: 1 -> 1, of which waited for: 1 -> 1; matrix products, arithmetic and copies ran while one was open for 1% -> 0% of each run, Pallas kernels for 0% -> 0%
where the time goes in v3:
time: 62.5 us; the launch traced here: 62.2 us
  blocking collectives  40.3 us (64%)
  starting transfers between devices  6.81 us (11%)
  Pallas kernels  6.46 us (10%)
  waiting for transfers between devices  6.37 us (10%)
  local copies, waits for them, and re-layouts  1.46 us (2%)
  between operations  0.67 us (1%)
    all_to_all x1, blocking collectives, shards(): arrived = lax.all_to_all(messages, 'band', 0, 0, tiled=True)  26.7 us
    all_to_all x1, blocking collectives, shards(): shares = lax.all_to_all(shares, 'band', 0, 0, tiled=True)  13.6 us
    all_to_all x1, starting transfers between devices, shards(): everyone = lax.all_to_all(sums, 'mem', 0, 0, tiled=True)  6.81 us
    all_to_all x1, waiting for transfers between devices, shards(): everyone = lax.all_to_all(sums, 'mem', 0, 0, tiled=True)  6.37 us
    pallas_call x1, Pallas kernels, to_messages(): pl.pallas_call(legendre_kernel, out_shape=jax.ShapeDtypeStruct((BANDS * S...  3.64 us
    pallas_call x1, Pallas kernels, to_grid(): pl.pallas_call(synthesis_kernel, out_shape=(jax.ShapeDtypeStruct((FIELDS,...  2.81 us
  transfers between devices with their start and end apart: 1, of which 1 were waited for; matrix products, arithmetic and copies ran while one was open for 0% of the time, Pallas kernels for 0%

profile of v3, /device:TPU:1, one launch (start us, length us, event | category | flops | bytes accessed | tf_op | source)
XLA Modules:
  0.0 62.2 jit_solution(535116729457526790)
XLA Ops:
  0.6 0.0 copy-start
  0.6 3.6 %shard_map.77 = bf16[768,128]{1,0:T(8,128)(2,1)S(1)} custom-call(s32[10]{0:T(128)} %waves_hbm.1, s32[1,64]{1,0:T(1,128)} %bitcast.18, bf16[16,2,14080]{2,1,0:T(2,128)(2,1)} %bitcast.15, bf16[40,14080]{1,0:T(8,128)(2,1)} %legendre_hbm.1), custom_call_target="tpu_custom_call" | custom-call | tf_op jit(solution)/shard_map/pallas_call | solution.py:231
  4.3 26.7 %all_to_all.20 = bf16[64,6,2,128]{3,2,1,0:T(2,128)(2,1)S(1)} all-to-all(bf16[64,6,2,128]{3,2,1,0:T(2,128)(2,1)S(1)} %bitcast.13), channel_id=1, replica_groups=mesh['band'=64,'mem'=8] {'band'}, dimensions={0} | all-to-all | bytes 393216 | tf_op jit(solution)/shard_map/all_to_all | solution.py:280
  31.0 0.0 copy-done
  31.0 2.8 %shard_map.78 = (bf16[16,2,2560]{2,1,0:T(2,128)(2,1)}, f32[64,64]{1,0:T(8,128)S(1)}) custom-call(bf16[768,128]{1,0:T(8,128)(2,1)S(1)} %bitcast.12, bf16[10,256,256]{2,1,0:T(8,128)(2,1)} %constant.7.clone.table_hbm, bf16[2,2560,256]{2,1,0:T(8,128)(2,1)S(1)} %copy-done), custom_call_target="tpu_custom_call" | custom-call | tf_op jit(solution)/shard_map/pallas_call | solution.py:250
  33.8 13.6 %all_to_all.21 = f32[64,1,64]{2,1,0:T(1,128)S(1)} all-to-all(f32[64,1,64]{2,1,0:T(1,128)S(1)} %bitcast.14), channel_id=1, replica_groups=mesh['band'=64,'mem'=8] {'band'}, dimensions={0} | all-to-all | bytes 32768 | tf_op jit(solution)/shard_map/all_to_all | solution.py:283
  47.4 0.1 reduce_sum.27
  47.5 0.6 broadcast_in_dim.2
  48.1 6.8 %all-to-all-start.2 = ((f32[8,1,64]{2,1,0:T(1,128)}), f32[8,1,64]{2,1,0:T(1,128)S(1)}, u32[]{:S(2)}, u32[]{:S(2)}) async-start(f32[8,1,64]{2,1,0:T(1,128)} %broadcast_in_dim.2), calls=%async_computation.2 | async-start | bytes 8192 | tf_op jit(solution)/shard_map/all_to_all | solution.py:286
  54.9 0.1 slice.3
  55.0 6.4 %all-to-all-done.2 = f32[8,1,64]{2,1,0:T(1,128)S(1)} async-done(((f32[8,1,64]{2,1,0:T(1,128)}), f32[8,1,64]{2,1,0:T(1,128)S(1)}, u32[]{:S(2)}, u32[]{:S(2)}) %all-to-all-start.2) | async-done | bytes 2080 | tf_op jit(solution)/shard_map/all_to_all | solution.py:286
  61.4 0.1 reshape.43
  61.5 0.7 %copy.15 = f32[2,8,4]{2,1,0:T(8,128)} copy(f32[2,8,4]{1,0,2:T(2,128)S(1)} %subtract_bitcast_fusion) | data formatting | bytes 512 | tf_op jit(solution)/shard_map/transpose | solution.py:290
  (4 shorter events, 0.1 us)
Async XLA Ops:
  0.6 30.3 %copy-start = (bf16[2,2560,256]{2,1,0:T(8,128)(2,1)S(1)}, bf16[2,2560,256]{2,1,0:T(8,128)(2,1)}, u32[]{:S(2)}) copy-start(bf16[2,2560,256]{2,1,0:T(8,128)(2,1)} %basis.1) | copy-start | bytes 7864324
  48.1 13.3 %all-to-all-start.2 = ((f32[8,1,64]{2,1,0:T(1,128)}), f32[8,1,64]{2,1,0:T(1,128)S(1)}, u32[]{:S(2)}, u32[]{:S(2)}) async-start(f32[8,1,64]{2,1,0:T(1,128)} %broadcast_in_dim.2), calls=%async_computation.2 | async-start | bytes 8192 | tf_op jit(solution)/shard_map/all_to_all | solution.py:286

commit v4 on v3

--- a/solution.py
+++ b/solution.py
@@ -45,7 +45,7 @@
 
 
 def legendre_kernel(
-    waves_hbm, lengths_hbm, spectra_hbm, legendre_hbm, out,
+    waves_hbm, lengths_hbm, spectra_hbm, legendre_hbm, table_hbm, out, table,
     waves, lengths, spectra_buf, legendre_buf, flat, sems, small_sems,
 ):
     waves_copy = pltpu.make_async_copy(waves_hbm, waves, small_sems.at[0])
@@ -66,6 +66,8 @@
         ]
     for load in loads:
         load.start()
+    table_copy = pltpu.make_async_copy(table_hbm, table, small_sems.at[2])
+    table_copy.start()
     waves_copy.wait()
     lengths_copy.wait()
     counts = lengths[...].astype(F32)
@@ -104,36 +106,29 @@
         north = legendre_buf[:, window]
         rows = jnp.concatenate([north, north * alternate], axis=0)
         fourier = lax.dot_general(
-            rows, masked, (((1,), (1,)), ((), ())), preferred_element_type=F32
+            masked, rows, (((1,), (1,)), ((), ())), preferred_element_type=F32
         )
-        if p % 2 == 0:
-            first = fourier
+        every = ([] if p == 0 else every) + [fourier]
+        if p < PAIRS - 1:
             continue
-        couple = jnp.concatenate([first, fourier], axis=1).astype(BF16)
-        picked = jnp.dot(pick, couple, preferred_element_type=F32)
+        couple = jnp.concatenate(every, axis=0).astype(BF16)
+        picked = lax.dot_general(
+            pick, couple, (((1,), (1,)), ((), ())), preferred_element_type=F32
+        )
         top, bottom = picked[:BANDS], picked[BANDS:]
-        flat[pl.ds(p - 1, BANDS, stride=SLOT_ROWS), :] = jnp.concatenate(
-            [top[:, :half], bottom[:, :half]], axis=1
-        )
-        flat[pl.ds(p, BANDS, stride=SLOT_ROWS), :] = jnp.concatenate(
-            [top[:, half:], bottom[:, half:]], axis=1
-        )
+        for i in range(PAIRS):
+            flat[pl.ds(i, BANDS, stride=SLOT_ROWS), :] = jnp.concatenate(
+                [top[:, i * half : (i + 1) * half], bottom[:, i * half : (i + 1) * half]], axis=1
+            )
     flat[pl.ds(PAIRS, BANDS, stride=SLOT_ROWS), :] = notes
     out[...] = flat[...].astype(BF16)
+    table_copy.wait()
 
 
 def synthesis_kernel(
-    arrived, table_hbm, basis, grid_out, share_out,
-    flat, sorted_buf, series, partial_buf, turned, table, sems,
+    arrived, table, basis, grid_out, share_out,
+    flat, sorted_buf, series, partial_buf, turned,
 ):
-    loads = [
-        pltpu.make_async_copy(
-            table_hbm.at[pl.ds(i, 2)], table.at[pl.ds(i, 2)], sems.at[i // 2]
-        )
-        for i in range(0, RADIX, 2)
-    ]
-    for load in loads:
-        load.start()
     flat[...] = arrived[...].astype(F32)
     notes = flat[pl.ds(PAIRS, BANDS, stride=SLOT_ROWS), :]
     keep = notes[0:1, KEEP_LANE : KEEP_LANE + 1]
@@ -159,8 +154,6 @@
                         a, pl.ds(r * 64 + h * 32 + c, FIELDS, stride=2), :
                     ]
     first = lax.broadcasted_iota(jnp.int32, (2 * FIELDS, BLK), 1) < PER_CLASS
-    for load in loads:
-        load.wait()
     real, imag = [], []
     for cls in range(RADIX):
         a = cls // 2
@@ -201,16 +194,20 @@
             pieces[5 + q] = (cos_even - cos_odd) - (sin_even - sin_odd)
     second = lax.broadcasted_iota(jnp.int32, (2 * FIELDS, STEP), 0) % 2
     kept = keep > 0.5
-    total = jnp.zeros((2 * FIELDS, MODES), F32)
+    uppers, lowers = [], []
     for q in range(RADIX):
-        window = slice(q * STEP, (q + 1) * STEP)
         upper_row = jnp.where(second == 0, pieces[q], 0.0)
         lower_row = jnp.where((second == 1) & kept, pieces[q], 0.0)
-        grid_out[:, :, window] = (
+        grid_out[:, :, q * STEP : (q + 1) * STEP] = (
             (upper_row + lower_row).astype(BF16).reshape(FIELDS, 2, STEP)
         )
-        total += jnp.dot(upper_row.astype(BF16), basis[0, window, :], preferred_element_type=F32)
-        total += jnp.dot(lower_row.astype(BF16), basis[1, window, :], preferred_element_type=F32)
+        uppers.append(upper_row.astype(BF16))
+        lowers.append(lower_row.astype(BF16))
+    total = jnp.dot(
+        jnp.concatenate(uppers + lowers, axis=1),
+        basis[...].reshape(2 * LON, MODES),
+        preferred_element_type=F32,
+    )
     for i in range(MODES // BLK):
         partial_buf[i] = total[:, i * BLK : (i + 1) * BLK]
         turned[i * BLK : (i + 1) * BLK, :FIELDS] = (
@@ -227,12 +224,15 @@
 PARAMS = pltpu.CompilerParams(vmem_limit_bytes=48 * 1024 * 1024)
 
 
-def to_messages(waves, lengths, spectra, legendre):
+def to_messages(waves, lengths, spectra, legendre, table):
     return pl.pallas_call(
         legendre_kernel,
-        out_shape=jax.ShapeDtypeStruct((BANDS * SLOT_ROWS, BLK), BF16),
-        in_specs=[HBM, HBM, HBM, HBM],
-        out_specs=VMEM,
+        out_shape=(
+            jax.ShapeDtypeStruct((BANDS * SLOT_ROWS, BLK), BF16),
+            jax.ShapeDtypeStruct((RADIX, STEP, STEP), BF16),
+        ),
+        in_specs=[HBM, HBM, HBM, HBM, HBM],
+        out_specs=(VMEM, VMEM),
         scratch_shapes=[
             pltpu.SMEM((PAIRS,), jnp.int32),
             pltpu.VMEM((1, BANDS), jnp.int32),
@@ -240,10 +240,10 @@
             pltpu.VMEM((HALF, PAIRS * PAIR_LEN), BF16),
             pltpu.VMEM((BANDS * SLOT_ROWS, BLK), F32),
             pltpu.SemaphoreType.DMA((2, LOADS)),
-            pltpu.SemaphoreType.DMA((2,)),
+            pltpu.SemaphoreType.DMA((3,)),
         ],
         compiler_params=PARAMS,
-    )(*[pltpu.with_memory_space_constraint(x, pltpu.HBM) for x in (waves, lengths, spectra, legendre)])
+    )(*[pltpu.with_memory_space_constraint(x, pltpu.HBM) for x in (waves, lengths, spectra, legendre, table)])
 
 
 def to_grid(arrived, table, basis):
@@ -253,7 +253,7 @@
             jax.ShapeDtypeStruct((FIELDS, 2, LON), BF16),
             jax.ShapeDtypeStruct((BANDS, SHARE * FIELDS), F32),
         ),
-        in_specs=[VMEM, HBM, VMEM],
+        in_specs=[VMEM, VMEM, VMEM],
         out_specs=(VMEM, VMEM),
         scratch_shapes=[
             pltpu.VMEM((BANDS * SLOT_ROWS, BLK), F32),
@@ -261,29 +261,29 @@
             pltpu.VMEM((4, LOWS // BLK, 2 * FIELDS, BLK), F32),
             pltpu.VMEM((MODES // BLK, 2 * FIELDS, BLK), F32),
             pltpu.VMEM((MODES, BLK), F32),
-            pltpu.VMEM((RADIX, STEP, STEP), BF16),
-            pltpu.SemaphoreType.DMA((RADIX // 2,)),
         ],
         compiler_params=PARAMS,
-    )(arrived, pltpu.with_memory_space_constraint(table, pltpu.HBM), basis)
+    )(arrived, table, basis)
 
 
 def shards(spectra, legendre, pair_waves, band_lengths, eof_basis):
     ens, fields, levels, parts, slots = spectra.shape
-    messages = to_messages(
+    messages, table = to_messages(
         pair_waves,
         band_lengths.reshape(1, BANDS),
         spectra.reshape(FIELDS, parts, slots),
         legendre,
+        jnp.asarray(wave_table()),
     )
     messages = messages.reshape(BANDS, SLOT_ROWS // 2, 2, BLK)
     arrived = lax.all_to_all(messages, "band", 0, 0, tiled=True)
     arrived = arrived.reshape(BANDS * SLOT_ROWS, BLK)
-    grid, shares = to_grid(arrived, jnp.asarray(wave_table()), eof_basis)
+    grid, shares = to_grid(arrived, table, eof_basis)
     shares = lax.all_to_all(shares, "band", 0, 0, tiled=True)
     groups = lax.axis_size("mem")
     sums = jnp.broadcast_to(jnp.sum(shares, axis=0)[None], (groups, SHARE * FIELDS))
     everyone = lax.all_to_all(sums, "mem", 0, 0, tiled=True)
+    everyone, sums = lax.optimization_barrier((everyone, sums))
     own = sums[0].reshape(SHARE, ens, fields * levels)
     total = jnp.sum(everyone, axis=0).reshape(SHARE, ens, fields * levels)
     mean = jnp.sum(total, axis=1, keepdims=True) / (ens * groups)

time: 62.5 us -> 60.3 us (0.965)
  blocking collectives: 40.3 us -> 53.5 us
  starting transfers between devices: 6.81 us -> 0 us
  waiting for transfers between devices: 6.37 us -> 0 us
  Pallas kernels: 6.46 us -> 4.98 us
    all_to_all x0 -> x1, blocking collectives: none -> 13.1 us  [shards(): everyone = lax.all_to_all(sums, 'mem', 0, 0, tiled=True)]
    all_to_all x1 -> x0, starting transfers between devices: 6.81 us -> none  [shards(): everyone = lax.all_to_all(sums, 'mem', 0, 0, tiled=True)]
    all_to_all x1 -> x0, waiting for transfers between devices: 6.37 us -> none  [shards(): everyone = lax.all_to_all(sums, 'mem', 0, 0, tiled=True)]
    pallas_call x1, Pallas kernels: 3.64 us -> 2.78 us  [to_messages(): pl.pallas_call(legendre_kernel, out_shape=(jax.ShapeDtypeStruct((BANDS *...]
  transfers between devices with their start and end apart: 1 -> 0, of which waited for: 1 -> 0; matrix products, arithmetic and copies ran while one was open for 0% -> 0% of each run, Pallas kernels for 0% -> 0%
where the time goes in v4:
time: 60.3 us; the launch traced here: 60.1 us
  blocking collectives  53.5 us (89%)
  Pallas kernels  4.98 us (8%)
  local copies, waits for them, and re-layouts  0.9 us (1%)
  between operations  0.67 us (1%)
    all_to_all x1, blocking collectives, shards(): arrived = lax.all_to_all(messages, 'band', 0, 0, tiled=True)  26.7 us
    all_to_all x1, blocking collectives, shards(): shares = lax.all_to_all(shares, 'band', 0, 0, tiled=True)  13.6 us
    all_to_all x1, blocking collectives, shards(): everyone = lax.all_to_all(sums, 'mem', 0, 0, tiled=True)  13.1 us
    pallas_call x1, Pallas kernels, to_messages(): pl.pallas_call(legendre_kernel, out_shape=(jax.ShapeDtypeStruct((BANDS *...  2.78 us
    pallas_call x1, Pallas kernels, to_grid(): pl.pallas_call(synthesis_kernel, out_shape=(jax.ShapeDtypeStruct((FIELDS,...  2.19 us

profile of v4, /device:TPU:1, one launch (start us, length us, event | category | flops | bytes accessed | tf_op | source)
XLA Modules:
  0.0 60.1 jit_solution(7810936694395148935)
XLA Ops:
  0.6 0.0 copy-start
  0.6 2.8 %shard_map.77 = (bf16[768,128]{1,0:T(8,128)(2,1)S(1)}, bf16[10,256,256]{2,1,0:T(8,128)(2,1)S(1)}) custom-call(s32[10]{0:T(128)} %waves_hbm.1, s32[1,64]{1,0:T(1,128)} %bitcast.18, bf16[16,2,14080]{2,1,0:T(2,128)(2,1)} %bitcast.15, bf16[40,14080]{1,0:T(8,128)(2,1)} %legendre_hbm.1, bf16[10,256,256]{2,1,0:T(8,128)(2,1)} %constant.7.clone.table_hbm), custom_call_target="tpu_custom_call" | custom-call | tf_op jit(solution)/shard_map/pallas_call | solution.py:228
  3.4 26.7 %all_to_all.23 = bf16[64,6,2,128]{3,2,1,0:T(2,128)(2,1)S(1)} all-to-all(bf16[64,6,2,128]{3,2,1,0:T(2,128)(2,1)S(1)} %bitcast.13), channel_id=1, replica_groups=mesh['band'=64,'mem'=8] {'band'}, dimensions={0} | all-to-all | bytes 393216 | tf_op jit(solution)/shard_map/all_to_all | solution.py:279
  30.1 0.0 copy-done
  30.1 2.2 %shard_map.78 = (bf16[16,2,2560]{2,1,0:T(2,128)(2,1)}, f32[64,64]{1,0:T(8,128)S(1)}) custom-call(bf16[768,128]{1,0:T(8,128)(2,1)S(1)} %bitcast.12, bf16[10,256,256]{2,1,0:T(8,128)(2,1)S(1)} %get-tuple-element.9.table, bf16[2,2560,256]{2,1,0:T(8,128)(2,1)S(1)} %copy-done), custom_call_target="tpu_custom_call" | custom-call | tf_op jit(solution)/shard_map/pallas_call | solution.py:250
  32.3 13.6 %all_to_all.24 = f32[64,1,64]{2,1,0:T(1,128)S(1)} all-to-all(f32[64,1,64]{2,1,0:T(1,128)S(1)} %bitcast.14), channel_id=1, replica_groups=mesh['band'=64,'mem'=8] {'band'}, dimensions={0} | all-to-all | bytes 32768 | tf_op jit(solution)/shard_map/all_to_all | solution.py:282
  45.9 0.1 reduce_sum.27
  46.0 13.1 %all_to_all.25 = f32[8,1,64]{2,1,0:T(1,128)S(1)} all-to-all(f32[8,1,64]{2,1,0:T(1,128)S(1)} %broadcast_in_dim.4), channel_id=1, replica_groups=mesh['band'=64,'mem'=8] {'mem'}, dimensions={0} | all-to-all | bytes 4096 | tf_op jit(solution)/shard_map/all_to_all | solution.py:285
  59.2 0.1 reshape.42
  59.4 0.1 reshape_squeeze.3
  59.4 0.7 %copy.10 = f32[2,8,4]{2,1,0:T(8,128)} copy(f32[2,8,4]{1,0,2:T(2,128)S(1)} %subtract_bitcast_fusion) | data formatting | bytes 512 | tf_op jit(solution)/shard_map/transpose | solution.py:290
  (7 shorter events, 0.1 us)
Async XLA Ops:
  0.6 29.5 %copy-start = (bf16[2,2560,256]{2,1,0:T(8,128)(2,1)S(1)}, bf16[2,2560,256]{2,1,0:T(8,128)(2,1)}, u32[]{:S(2)}) copy-start(bf16[2,2560,256]{2,1,0:T(8,128)(2,1)} %basis.1) | copy-start | bytes 7864324

commit v5 on v4

--- a/solution.py
+++ b/solution.py
@@ -88,10 +88,11 @@
     parity = lax.broadcasted_iota(jnp.int32, (HALF, PAIR_LEN), 1) % 2
     alternate = jnp.where(parity == 0, 1.0, -1.0).astype(BF16)
     flat[...] = jnp.zeros(flat.shape, F32)
-    for load in loads:
-        load.wait()
     half = BLK // 2
     for p in range(PAIRS):
+        if p % (PAIRS // LOADS) == 0:
+            for load in loads[2 * p * LOADS // PAIRS :][:2]:
+                load.wait()
         wave = waves[p]
         place = (wave % RADIX) * PER_CLASS + wave // RADIX
         notes = jnp.where(lane == p, (place // DIGIT).astype(F32), notes)
@@ -203,11 +204,9 @@
         )
         uppers.append(upper_row.astype(BF16))
         lowers.append(lower_row.astype(BF16))
-    total = jnp.dot(
-        jnp.concatenate(uppers + lowers, axis=1),
-        basis[...].reshape(2 * LON, MODES),
-        preferred_element_type=F32,
-    )
+    lhs = jnp.concatenate(uppers + lowers, axis=1)
+    rhs = basis[...].reshape(2 * LON, MODES)
+    total = jnp.concatenate([jnp.dot(lhs, rhs[:, i*128:(i+1)*128], preferred_element_type=F32) for i in range(2)], axis=1)
     for i in range(MODES // BLK):
         partial_buf[i] = total[:, i * BLK : (i + 1) * BLK]
         turned[i * BLK : (i + 1) * BLK, :FIELDS] = (

time: 60.3 us -> 59.7 us (0.990)
  no operation moved by 1% of the time
where the time goes in v5:
time: 59.7 us; the launch traced here: 59.5 us
  blocking collectives  53.4 us (89%)
  Pallas kernels  4.41 us (7%)
  local copies, waits for them, and re-layouts  0.9 us (2%)
  between operations  0.66 us (1%)
    all_to_all x1, blocking collectives, shards(): arrived = lax.all_to_all(messages, 'band', 0, 0, tiled=True)  26.7 us
    all_to_all x1, blocking collectives, shards(): shares = lax.all_to_all(shares, 'band', 0, 0, tiled=True)  13.6 us
    all_to_all x1, blocking collectives, shards(): everyone = lax.all_to_all(sums, 'mem', 0, 0, tiled=True)  13.1 us
    pallas_call x1, Pallas kernels, to_messages(): pl.pallas_call(legendre_kernel, out_shape=(jax.ShapeDtypeStruct((BANDS *...  2.69 us
    pallas_call x1, Pallas kernels, to_grid(): pl.pallas_call(synthesis_kernel, out_shape=(jax.ShapeDtypeStruct((FIELDS,...  1.72 us

profile of v5, /device:TPU:1, one launch (start us, length us, event | category | flops | bytes accessed | tf_op | source)
XLA Modules:
  0.0 59.5 jit_solution(3263107945305038138)
XLA Ops:
  0.6 0.0 copy-start
  0.6 2.7 %shard_map.77 = (bf16[768,128]{1,0:T(8,128)(2,1)S(1)}, bf16[10,256,256]{2,1,0:T(8,128)(2,1)S(1)}) custom-call(s32[10]{0:T(128)} %waves_hbm.1, s32[1,64]{1,0:T(1,128)} %bitcast.18, bf16[16,2,14080]{2,1,0:T(2,128)(2,1)} %bitcast.15, bf16[40,14080]{1,0:T(8,128)(2,1)} %legendre_hbm.1, bf16[10,256,256]{2,1,0:T(8,128)(2,1)} %constant.7.clone.table_hbm), custom_call_target="tpu_custom_call" | custom-call | tf_op jit(solution)/shard_map/pallas_call | solution.py:227
  3.3 26.7 %all_to_all.23 = bf16[64,6,2,128]{3,2,1,0:T(2,128)(2,1)S(1)} all-to-all(bf16[64,6,2,128]{3,2,1,0:T(2,128)(2,1)S(1)} %bitcast.13), channel_id=1, replica_groups=mesh['band'=64,'mem'=8] {'band'}, dimensions={0} | all-to-all | bytes 393216 | tf_op jit(solution)/shard_map/all_to_all | solution.py:278
  30.0 0.0 copy-done
  30.0 1.7 %shard_map.78 = (bf16[16,2,2560]{2,1,0:T(2,128)(2,1)}, f32[64,64]{1,0:T(8,128)S(1)}) custom-call(bf16[768,128]{1,0:T(8,128)(2,1)S(1)} %bitcast.12, bf16[10,256,256]{2,1,0:T(8,128)(2,1)S(1)} %get-tuple-element.9.table, bf16[2,2560,256]{2,1,0:T(8,128)(2,1)S(1)} %copy-done), custom_call_target="tpu_custom_call" | custom-call | tf_op jit(solution)/shard_map/pallas_call | solution.py:249
  31.7 13.6 %all_to_all.24 = f32[64,1,64]{2,1,0:T(1,128)S(1)} all-to-all(f32[64,1,64]{2,1,0:T(1,128)S(1)} %bitcast.14), channel_id=1, replica_groups=mesh['band'=64,'mem'=8] {'band'}, dimensions={0} | all-to-all | bytes 32768 | tf_op jit(solution)/shard_map/all_to_all | solution.py:281
  45.4 0.1 reduce_sum.27
  45.4 13.1 %all_to_all.25 = f32[8,1,64]{2,1,0:T(1,128)S(1)} all-to-all(f32[8,1,64]{2,1,0:T(1,128)S(1)} %broadcast_in_dim.4), channel_id=1, replica_groups=mesh['band'=64,'mem'=8] {'mem'}, dimensions={0} | all-to-all | bytes 4096 | tf_op jit(solution)/shard_map/all_to_all | solution.py:284
  58.6 0.1 reshape.42
  58.7 0.1 reshape_squeeze.3
  58.8 0.7 %copy.10 = f32[2,8,4]{2,1,0:T(8,128)} copy(f32[2,8,4]{1,0,2:T(2,128)S(1)} %subtract_bitcast_fusion) | data formatting | bytes 512 | tf_op jit(solution)/shard_map/transpose | solution.py:289
  (7 shorter events, 0.1 us)
Async XLA Ops:
  0.6 29.4 %copy-start = (bf16[2,2560,256]{2,1,0:T(8,128)(2,1)S(1)}, bf16[2,2560,256]{2,1,0:T(8,128)(2,1)}, u32[]{:S(2)}) copy-start(bf16[2,2560,256]{2,1,0:T(8,128)(2,1)} %basis.1) | copy-start | bytes 7864324

commit v6 on v5

--- a/solution.py
+++ b/solution.py
@@ -6,6 +6,7 @@
 from jax import lax
 from jax.experimental import pallas as pl
 from jax.experimental.pallas import tpu as pltpu
+from jax.sharding import Mesh
 from jax.sharding import PartitionSpec as P
 
 WAVE_COUNT = 1280
@@ -13,6 +14,7 @@
 BLK = 128
 HALF = 40
 BANDS = 64
+RING = 8
 PAIRS = 10
 PAIR_LEN = 1408
 FIELDS = 16
@@ -71,7 +73,8 @@
     waves_copy.wait()
     lengths_copy.wait()
     counts = lengths[...].astype(F32)
-    dest = lax.broadcasted_iota(jnp.int32, (BANDS, BANDS), 0)
+    order = lax.broadcasted_iota(jnp.int32, (BANDS, BANDS), 0)
+    dest = (order % RING) * (BANDS // RING) + order // RING
     other = lax.broadcasted_iota(jnp.int32, (BANDS, BANDS), 1)
     starts = jnp.sum(jnp.where(other < dest, counts, 0.0), axis=1, keepdims=True)
     own = jnp.sum(jnp.where(other == dest, counts, 0.0), axis=1, keepdims=True)
@@ -275,10 +278,10 @@
         jnp.asarray(wave_table()),
     )
     messages = messages.reshape(BANDS, SLOT_ROWS // 2, 2, BLK)
-    arrived = lax.all_to_all(messages, "band", 0, 0, tiled=True)
+    arrived = lax.all_to_all(messages, ("plane", "ring"), 0, 0, tiled=True)
     arrived = arrived.reshape(BANDS * SLOT_ROWS, BLK)
     grid, shares = to_grid(arrived, table, eof_basis)
-    shares = lax.all_to_all(shares, "band", 0, 0, tiled=True)
+    shares = lax.all_to_all(shares, ("ring", "plane"), 0, 0, tiled=True)
     groups = lax.axis_size("mem")
     sums = jnp.broadcast_to(jnp.sum(shares, axis=0)[None], (groups, SHARE * FIELDS))
     everyone = lax.all_to_all(sums, "mem", 0, 0, tiled=True)
@@ -291,16 +294,18 @@
 
 
 def solution(mesh):
+    devices = mesh.devices.reshape(RING, BANDS // RING, -1)
+    band = ("ring", "plane")
     return jax.shard_map(
         shards,
-        mesh=mesh,
+        mesh=Mesh(devices, (*band, "mem")),
         in_specs=(
-            P("mem", None, None, None, "band"),
-            P(None, "band"),
-            P("band"),
+            P("mem", None, None, None, band),
+            P(None, band),
+            P(band),
             P(),
-            P("band", None, None),
+            P(band, None, None),
         ),
-        out_specs=(P("mem", None, None, "band", None), P("mem", None, None, "band")),
+        out_specs=(P("mem", None, None, band, None), P("mem", None, None, band)),
         check_vma=False,
     )

time: 59.7 us -> 59.9 us (level)
  no operation moved by 1% of the time
where the time goes in v6:
time: 59.9 us; the launch traced here: 59.7 us
  blocking collectives  53.6 us (89%)
  Pallas kernels  4.4 us (7%)
  local copies, waits for them, and re-layouts  0.9 us (2%)
  between operations  0.66 us (1%)
    all_to_all x1, blocking collectives, shards(): arrived = lax.all_to_all(messages, ('plane', 'ring'), 0, 0, tiled=True)  25.4 us
    all_to_all x1, blocking collectives, shards(): shares = lax.all_to_all(shares, ('ring', 'plane'), 0, 0, tiled=True)  15 us
    all_to_all x1, blocking collectives, shards(): everyone = lax.all_to_all(sums, 'mem', 0, 0, tiled=True)  13.1 us
    pallas_call x1, Pallas kernels, to_messages(): pl.pallas_call(legendre_kernel, out_shape=(jax.ShapeDtypeStruct((BANDS *...  2.69 us
    pallas_call x1, Pallas kernels, to_grid(): pl.pallas_call(synthesis_kernel, out_shape=(jax.ShapeDtypeStruct((FIELDS,...  1.72 us

profile of v6, /device:TPU:1, one launch (start us, length us, event | category | flops | bytes accessed | tf_op | source)
XLA Modules:
  0.0 59.7 jit_solution(1555496299851921359)
XLA Ops:
  0.6 0.0 copy-start
  0.6 2.7 %shard_map.77 = (bf16[768,128]{1,0:T(8,128)(2,1)S(1)}, bf16[10,256,256]{2,1,0:T(8,128)(2,1)S(1)}) custom-call(s32[10]{0:T(128)} %waves_hbm.1, s32[1,64]{1,0:T(1,128)} %bitcast.18, bf16[16,2,14080]{2,1,0:T(2,128)(2,1)} %bitcast.15, bf16[40,14080]{1,0:T(8,128)(2,1)} %legendre_hbm.1, bf16[10,256,256]{2,1,0:T(8,128)(2,1)} %constant.7.clone.table_hbm), custom_call_target="tpu_custom_call" | custom-call | tf_op jit(solution)/shard_map/pallas_call | solution.py:230
  3.3 25.4 %all_to_all.23 = bf16[64,6,2,128]{3,2,1,0:T(2,128)(2,1)S(1)} all-to-all(bf16[64,6,2,128]{3,2,1,0:T(2,128)(2,1)S(1)} %bitcast.13), channel_id=1, replica_groups=mesh['ring'=8,'plane'=8,'mem'=8] {'plane','ring'}, dimensions={0} | all-to-all | bytes 393216 | tf_op jit(solution)/shard_map/all_to_all | solution.py:281
  28.8 0.0 copy-done
  28.8 1.7 %shard_map.78 = (bf16[16,2,2560]{2,1,0:T(2,128)(2,1)}, f32[64,64]{1,0:T(8,128)S(1)}) custom-call(bf16[768,128]{1,0:T(8,128)(2,1)S(1)} %bitcast.12, bf16[10,256,256]{2,1,0:T(8,128)(2,1)S(1)} %get-tuple-element.9.table, bf16[2,2560,256]{2,1,0:T(8,128)(2,1)S(1)} %copy-done), custom_call_target="tpu_custom_call" | custom-call | tf_op jit(solution)/shard_map/pallas_call | solution.py:252
  30.5 15.0 %all_to_all.24 = f32[64,1,64]{2,1,0:T(1,128)S(1)} all-to-all(f32[64,1,64]{2,1,0:T(1,128)S(1)} %bitcast.14), channel_id=1, replica_groups=mesh['ring'=8,'plane'=8,'mem'=8] {'ring','plane'}, dimensions={0} | all-to-all | bytes 32768 | tf_op jit(solution)/shard_map/all_to_all | solution.py:284
  45.5 0.1 reduce_sum.27
  45.6 13.1 %all_to_all.25 = f32[8,1,64]{2,1,0:T(1,128)S(1)} all-to-all(f32[8,1,64]{2,1,0:T(1,128)S(1)} %broadcast_in_dim.4), channel_id=1, replica_groups=mesh['ring'=8,'plane'=8,'mem'=8] {'mem'}, dimensions={0} | all-to-all | bytes 4096 | tf_op jit(solution)/shard_map/all_to_all | solution.py:287
  58.8 0.1 reshape.42
  58.9 0.1 reshape_squeeze.3
  59.0 0.7 %copy.10 = f32[2,8,4]{2,1,0:T(8,128)} copy(f32[2,8,4]{1,0,2:T(2,128)S(1)} %subtract_bitcast_fusion) | data formatting | bytes 512 | tf_op jit(solution)/shard_map/transpose | solution.py:292
  (7 shorter events, 0.1 us)
Async XLA Ops:
  0.6 28.1 %copy-start = (bf16[2,2560,256]{2,1,0:T(8,128)(2,1)S(1)}, bf16[2,2560,256]{2,1,0:T(8,128)(2,1)}, u32[]{:S(2)}) copy-start(bf16[2,2560,256]{2,1,0:T(8,128)(2,1)} %basis.1) | copy-start | bytes 7864324

commit v7 on v5

--- a/solution.py
+++ b/solution.py
@@ -24,7 +24,7 @@
 LOADS = 2
 LOWS = WAVE_COUNT // 2
 PER_CLASS = LOWS // RADIX
-DIGIT = 16
+DIGIT = 128
 KEEP_LANE = 2 * PAIRS
 F32 = jnp.float32
 BF16 = jnp.bfloat16
@@ -133,21 +133,26 @@
     flat[...] = arrived[...].astype(F32)
     notes = flat[pl.ds(PAIRS, BANDS, stride=SLOT_ROWS), :]
     keep = notes[0:1, KEEP_LANE : KEEP_LANE + 1]
-    target = lax.broadcasted_iota(jnp.int32, (BANDS, LOWS), 1).astype(F32)
+    target = lax.broadcasted_iota(jnp.int32, (BANDS, BLK), 1).astype(F32)
+    blocks = notes.T
     sources, hits = [], []
     for p in range(0, PAIRS, 2):
         couple = [flat[pl.ds(p + i, BANDS, stride=SLOT_ROWS), :] for i in range(2)]
         sources.append(jnp.concatenate(couple, axis=0).T.astype(BF16))
     for p in range(PAIRS):
-        place = DIGIT * notes[:, p : p + 1] + notes[:, PAIRS + p : PAIRS + p + 1]
-        hits.append(jnp.where(target == place, 1.0, 0.0).astype(BF16))
-    by_wave = jnp.dot(
-        jnp.concatenate(sources, axis=1),
-        jnp.concatenate(hits, axis=0),
-        preferred_element_type=F32,
-    )
+        hits.append(
+            jnp.where(target == notes[:, PAIRS + p : PAIRS + p + 1], 1.0, 0.0).astype(BF16)
+        )
+    source = jnp.concatenate(sources, axis=1)
+    block = jnp.concatenate([blocks[p : p + 1, :BANDS] for p in range(PAIRS)], axis=1)
+    block = jnp.broadcast_to(block, (FIELDS, LOWS))
+    stacked = []
     for a in range(LOWS // BLK):
-        sorted_buf[a] = by_wave[:, a * BLK : (a + 1) * BLK]
+        mine = jnp.where(block == a, 1.0, 0.0).astype(BF16)
+        stacked.append(source * jnp.concatenate([mine] * (BLK // FIELDS), axis=0))
+    hit = jnp.concatenate(hits, axis=0)
+    for a in range(LOWS // BLK):
+        sorted_buf[a] = jnp.dot(stacked[a], hit, preferred_element_type=F32)
         for h in range(2):
             for c in range(2):
                 for r in range(2):
@@ -206,7 +211,7 @@
         lowers.append(lower_row.astype(BF16))
     lhs = jnp.concatenate(uppers + lowers, axis=1)
     rhs = basis[...].reshape(2 * LON, MODES)
-    total = jnp.concatenate([jnp.dot(lhs, rhs[:, i*128:(i+1)*128], preferred_element_type=F32) for i in range(2)], axis=1)
+    total = jnp.concatenate([sum(jnp.dot(lhs[:, k*1280:(k+1)*1280], rhs[k*1280:(k+1)*1280, i*128:(i+1)*128], preferred_element_type=F32) for k in range(4)) for i in range(2)], axis=1)
     for i in range(MODES // BLK):
         partial_buf[i] = total[:, i * BLK : (i + 1) * BLK]
         turned[i * BLK : (i + 1) * BLK, :FIELDS] = (

time: 59.7 us -> 59.7 us (level)
  no operation moved by 1% of the time
where the time goes in v7:
time: 59.7 us; the launch traced here: 59.5 us
  blocking collectives  53.4 us (89%)
  Pallas kernels  4.38 us (7%)
  local copies, waits for them, and re-layouts  0.9 us (2%)
  between operations  0.66 us (1%)
    all_to_all x1, blocking collectives, shards(): arrived = lax.all_to_all(messages, 'band', 0, 0, tiled=True)  26.7 us
    all_to_all x1, blocking collectives, shards(): shares = lax.all_to_all(shares, 'band', 0, 0, tiled=True)  13.6 us
    all_to_all x1, blocking collectives, shards(): everyone = lax.all_to_all(sums, 'mem', 0, 0, tiled=True)  13.1 us
    pallas_call x1, Pallas kernels, to_messages(): pl.pallas_call(legendre_kernel, out_shape=(jax.ShapeDtypeStruct((BANDS *...  2.69 us
    pallas_call x1, Pallas kernels, to_grid(): pl.pallas_call(synthesis_kernel, out_shape=(jax.ShapeDtypeStruct((FIELDS,...  1.7 us

profile of v7, /device:TPU:1, one launch (start us, length us, event | category | flops | bytes accessed | tf_op | source)
XLA Modules:
  0.0 59.5 jit_solution(5038477013320368883)
XLA Ops:
  0.6 0.0 copy-start
  0.6 2.7 %shard_map.77 = (bf16[768,128]{1,0:T(8,128)(2,1)S(1)}, bf16[10,256,256]{2,1,0:T(8,128)(2,1)S(1)}) custom-call(s32[10]{0:T(128)} %waves_hbm.1, s32[1,64]{1,0:T(1,128)} %bitcast.18, bf16[16,2,14080]{2,1,0:T(2,128)(2,1)} %bitcast.15, bf16[40,14080]{1,0:T(8,128)(2,1)} %legendre_hbm.1, bf16[10,256,256]{2,1,0:T(8,128)(2,1)} %constant.7.clone.table_hbm), custom_call_target="tpu_custom_call" | custom-call | tf_op jit(solution)/shard_map/pallas_call | solution.py:232
  3.3 26.7 %all_to_all.23 = bf16[64,6,2,128]{3,2,1,0:T(2,128)(2,1)S(1)} all-to-all(bf16[64,6,2,128]{3,2,1,0:T(2,128)(2,1)S(1)} %bitcast.13), channel_id=1, replica_groups=mesh['band'=64,'mem'=8] {'band'}, dimensions={0} | all-to-all | bytes 393216 | tf_op jit(solution)/shard_map/all_to_all | solution.py:283
  30.0 0.0 copy-done
  30.0 1.7 %shard_map.78 = (bf16[16,2,2560]{2,1,0:T(2,128)(2,1)}, f32[64,64]{1,0:T(8,128)S(1)}) custom-call(bf16[768,128]{1,0:T(8,128)(2,1)S(1)} %bitcast.12, bf16[10,256,256]{2,1,0:T(8,128)(2,1)S(1)} %get-tuple-element.9.table, bf16[2,2560,256]{2,1,0:T(8,128)(2,1)S(1)} %copy-done), custom_call_target="tpu_custom_call" | custom-call | tf_op jit(solution)/shard_map/pallas_call | solution.py:254
  31.7 13.6 %all_to_all.24 = f32[64,1,64]{2,1,0:T(1,128)S(1)} all-to-all(f32[64,1,64]{2,1,0:T(1,128)S(1)} %bitcast.14), channel_id=1, replica_groups=mesh['band'=64,'mem'=8] {'band'}, dimensions={0} | all-to-all | bytes 32768 | tf_op jit(solution)/shard_map/all_to_all | solution.py:286
  45.3 0.1 reduce_sum.27
  45.4 13.1 %all_to_all.25 = f32[8,1,64]{2,1,0:T(1,128)S(1)} all-to-all(f32[8,1,64]{2,1,0:T(1,128)S(1)} %broadcast_in_dim.4), channel_id=1, replica_groups=mesh['band'=64,'mem'=8] {'mem'}, dimensions={0} | all-to-all | bytes 4096 | tf_op jit(solution)/shard_map/all_to_all | solution.py:289
  58.6 0.1 reshape.42
  58.7 0.1 reshape_squeeze.3
  58.8 0.7 %copy.10 = f32[2,8,4]{2,1,0:T(8,128)} copy(f32[2,8,4]{1,0,2:T(2,128)S(1)} %subtract_bitcast_fusion) | data formatting | bytes 512 | tf_op jit(solution)/shard_map/transpose | solution.py:294
  (7 shorter events, 0.1 us)
Async XLA Ops:
  0.6 29.4 %copy-start = (bf16[2,2560,256]{2,1,0:T(8,128)(2,1)S(1)}, bf16[2,2560,256]{2,1,0:T(8,128)(2,1)}, u32[]{:S(2)}) copy-start(bf16[2,2560,256]{2,1,0:T(8,128)(2,1)} %basis.1) | copy-start | bytes 7864324

commit v8 on v7

--- a/solution.py
+++ b/solution.py
@@ -6,6 +6,7 @@
 from jax import lax
 from jax.experimental import pallas as pl
 from jax.experimental.pallas import tpu as pltpu
+from jax.sharding import Mesh
 from jax.sharding import PartitionSpec as P
 
 WAVE_COUNT = 1280
@@ -71,7 +72,8 @@
     waves_copy.wait()
     lengths_copy.wait()
     counts = lengths[...].astype(F32)
-    dest = lax.broadcasted_iota(jnp.int32, (BANDS, BANDS), 0)
+    order = lax.broadcasted_iota(jnp.int32, (BANDS, BANDS), 0)
+    dest = order // 8 * 8 + order % 4 * 2 + order // 4 % 2
     other = lax.broadcasted_iota(jnp.int32, (BANDS, BANDS), 1)
     starts = jnp.sum(jnp.where(other < dest, counts, 0.0), axis=1, keepdims=True)
     own = jnp.sum(jnp.where(other == dest, counts, 0.0), axis=1, keepdims=True)
@@ -280,10 +282,10 @@
         jnp.asarray(wave_table()),
     )
     messages = messages.reshape(BANDS, SLOT_ROWS // 2, 2, BLK)
-    arrived = lax.all_to_all(messages, "band", 0, 0, tiled=True)
+    arrived = lax.all_to_all(messages, ("z", "core", "x"), 0, 0, tiled=True)
     arrived = arrived.reshape(BANDS * SLOT_ROWS, BLK)
     grid, shares = to_grid(arrived, table, eof_basis)
-    shares = lax.all_to_all(shares, "band", 0, 0, tiled=True)
+    shares = lax.all_to_all(shares, ("z", "x", "core"), 0, 0, tiled=True)
     groups = lax.axis_size("mem")
     sums = jnp.broadcast_to(jnp.sum(shares, axis=0)[None], (groups, SHARE * FIELDS))
     everyone = lax.all_to_all(sums, "mem", 0, 0, tiled=True)
@@ -296,16 +298,17 @@
 
 
 def solution(mesh):
+    band = ("z", "x", "core")
     return jax.shard_map(
         shards,
-        mesh=mesh,
+        mesh=Mesh(mesh.devices.reshape(8, 4, 2, -1), (*band, "mem")),
         in_specs=(
-            P("mem", None, None, None, "band"),
-            P(None, "band"),
-            P("band"),
+            P("mem", None, None, None, band),
+            P(None, band),
+            P(band),
             P(),
-            P("band", None, None),
+            P(band, None, None),
         ),
-        out_specs=(P("mem", None, None, "band", None), P("mem", None, None, "band")),
+        out_specs=(P("mem", None, None, band, None), P("mem", None, None, band)),
         check_vma=False,
     )

time: 59.7 us -> 59.7 us (level)
  no operation moved by 1% of the time
where the time goes in v8:
time: 59.7 us; the launch traced here: 59.5 us
  blocking collectives  53.4 us (89%)
  Pallas kernels  4.38 us (7%)
  local copies, waits for them, and re-layouts  0.9 us (2%)
  between operations  0.66 us (1%)
    all_to_all x1, blocking collectives, shards(): arrived = lax.all_to_all(messages, ('z', 'core', 'x'), 0, 0, tiled=True)  25.6 us
    all_to_all x1, blocking collectives, shards(): shares = lax.all_to_all(shares, ('z', 'x', 'core'), 0, 0, tiled=True)  14.7 us
    all_to_all x1, blocking collectives, shards(): everyone = lax.all_to_all(sums, 'mem', 0, 0, tiled=True)  13.1 us
    pallas_call x1, Pallas kernels, to_messages(): pl.pallas_call(legendre_kernel, out_shape=(jax.ShapeDtypeStruct((BANDS *...  2.69 us
    pallas_call x1, Pallas kernels, to_grid(): pl.pallas_call(synthesis_kernel, out_shape=(jax.ShapeDtypeStruct((FIELDS,...  1.7 us

profile of v8, /device:TPU:1, one launch (start us, length us, event | category | flops | bytes accessed | tf_op | source)
XLA Modules:
  0.0 59.5 jit_solution(10111006569291222887)
XLA Ops:
  0.6 0.0 copy-start
  0.6 2.7 %shard_map.77 = (bf16[768,128]{1,0:T(8,128)(2,1)S(1)}, bf16[10,256,256]{2,1,0:T(8,128)(2,1)S(1)}) custom-call(s32[10]{0:T(128)} %waves_hbm.1, s32[1,64]{1,0:T(1,128)} %bitcast.18, bf16[16,2,14080]{2,1,0:T(2,128)(2,1)} %bitcast.15, bf16[40,14080]{1,0:T(8,128)(2,1)} %legendre_hbm.1, bf16[10,256,256]{2,1,0:T(8,128)(2,1)} %constant.7.clone.table_hbm), custom_call_target="tpu_custom_call" | custom-call | tf_op jit(solution)/shard_map/pallas_call | solution.py:234
  3.3 25.6 %all_to_all.23 = bf16[64,6,2,128]{3,2,1,0:T(2,128)(2,1)S(1)} all-to-all(bf16[64,6,2,128]{3,2,1,0:T(2,128)(2,1)S(1)} %bitcast.13), channel_id=1, replica_groups=mesh['z'=8,'x'=4,'core'=2,'mem'=8] {'z','core','x'}, dimensions={0} | all-to-all | bytes 393216 | tf_op jit(solution)/shard_map/all_to_all | solution.py:285
  28.9 0.0 copy-done
  29.0 1.7 %shard_map.78 = (bf16[16,2,2560]{2,1,0:T(2,128)(2,1)}, f32[64,64]{1,0:T(8,128)S(1)}) custom-call(bf16[768,128]{1,0:T(8,128)(2,1)S(1)} %bitcast.12, bf16[10,256,256]{2,1,0:T(8,128)(2,1)S(1)} %get-tuple-element.9.table, bf16[2,2560,256]{2,1,0:T(8,128)(2,1)S(1)} %copy-done), custom_call_target="tpu_custom_call" | custom-call | tf_op jit(solution)/shard_map/pallas_call | solution.py:256
  30.6 14.7 %all_to_all.24 = f32[64,1,64]{2,1,0:T(1,128)S(1)} all-to-all(f32[64,1,64]{2,1,0:T(1,128)S(1)} %bitcast.14), channel_id=1, replica_groups=mesh['z'=8,'x'=4,'core'=2,'mem'=8] {'z','x','core'}, dimensions={0} | all-to-all | bytes 32768 | tf_op jit(solution)/shard_map/all_to_all | solution.py:288
  45.3 0.1 reduce_sum.27
  45.4 13.1 %all_to_all.25 = f32[8,1,64]{2,1,0:T(1,128)S(1)} all-to-all(f32[8,1,64]{2,1,0:T(1,128)S(1)} %broadcast_in_dim.4), channel_id=1, replica_groups=mesh['z'=8,'x'=4,'core'=2,'mem'=8] {'mem'}, dimensions={0} | all-to-all | bytes 4096 | tf_op jit(solution)/shard_map/all_to_all | solution.py:291
  58.6 0.1 reshape.42
  58.7 0.1 reshape_squeeze.3
  58.8 0.7 %copy.10 = f32[2,8,4]{2,1,0:T(8,128)} copy(f32[2,8,4]{1,0,2:T(2,128)S(1)} %subtract_bitcast_fusion) | data formatting | bytes 512 | tf_op jit(solution)/shard_map/transpose | solution.py:296
  (7 shorter events, 0.1 us)
Async XLA Ops:
  0.6 28.3 %copy-start = (bf16[2,2560,256]{2,1,0:T(8,128)(2,1)S(1)}, bf16[2,2560,256]{2,1,0:T(8,128)(2,1)}, u32[]{:S(2)}) copy-start(bf16[2,2560,256]{2,1,0:T(8,128)(2,1)} %basis.1) | copy-start | bytes 7864324
